TPU v7x, 256 devices: a whole 4x4x8 slice. The times are simulated.
256 devices in a mesh: row: 16 (over z, core), col: 16 (over y, x).
Axes of the slice: x: 4, y: 4, z: 8, core: 2. Of those that a mesh axis runs over, the one named last changes fastest.
Arguments:
- matrix: float32 [8192, 8192], P('row', 'col'), as said below
Outputs:
- reduced: float32 [8192, 8192], P('row', 'col')
Inputs may be any that keep to these rules, and one draw needn't show every extreme that they name: matrix is symmetric.
All inputs are finite; a program needn't handle non-finite values.
Results may differ from a plain program's by a relative error of at most 0.00014.
Values sent between devices are 32-bit elements; how exact they have to be, the bound alone decides.
A program may use at most 64 MiB of HBM per device.

v0:
```python
import jax
import jax.numpy as jnp
from jax import lax
from jax.sharding import PartitionSpec as P

BLOCK = 256
PANELS = 2


HIGH = lax.Precision.HIGHEST


def broadcast(block, axis, source):
    block = jnp.where(lax.axis_index(axis) == source, block, jnp.zeros_like(block))
    return lax.psum(block, axis)


def mult(left, right):
    return jnp.dot(left, right, precision=HIGH, preferred_element_type=jnp.float32)


def inverse_transposed(shifted):
    factor = jnp.linalg.cholesky(mult(shifted, shifted.T))
    half = jax.scipy.linalg.solve_triangular(factor, shifted, lower=True)
    return jax.scipy.linalg.solve_triangular(factor, half, lower=True, trans="T")


def reflector_columns(local_rows, column, ratio):
    pieces = broadcast(local_rows, "row", column * ratio + 0)
    return pieces


def update_columns(local_rows, column, ratio):
    pieces = broadcast(local_rows, "row", column * ratio + 0)
    return pieces


def reflect(current, index, row_index, column, ratio):
    height = current.shape[0]
    lead = (index + 1) * BLOCK
    owner = lead // height
    offset_top = lead - owner * height
    rows = row_index * height + jnp.arange(height, dtype=jnp.int32)
    local_panel = jnp.where(
        (rows >= lead)[:, None], current[:, index * BLOCK : (index + 1) * BLOCK], jnp.float32(0.0)
    )
    panel = broadcast(local_panel, "col", 0)
    local_gram = mult(panel.T, panel)
    gram = lax.psum(local_gram, "row")
    top_panel = broadcast(panel[offset_top : offset_top + BLOCK], "row", owner)
    lower = jnp.linalg.cholesky(gram)
    basis = jax.scipy.linalg.solve_triangular(lower, panel.T, lower=True).T
    top = jax.scipy.linalg.solve_triangular(lower, top_panel.T, lower=True).T
    kernel = inverse_transposed(jnp.eye(BLOCK, dtype=jnp.float32) + top)
    unit = ((rows - lead)[:, None] == jnp.arange(BLOCK, dtype=jnp.int32)[None, :]).astype(
        jnp.float32
    )
    vectors = basis + unit
    vectors_cols = reflector_columns(vectors, column, ratio)
    product = lax.psum(mult(current, vectors_cols), "col")
    inner = lax.psum(mult(vectors.T, product), "row")
    coupled = mult(kernel.T, mult(inner, kernel))
    update = mult(product, kernel) - 0.5 * mult(vectors, coupled)
    update_cols = update_columns(update, column, ratio)
    return current - mult(update, vectors_cols.T) - mult(vectors, update_cols.T)


def per_device(matrix):
    row_index = lax.axis_index("row")
    column = lax.axis_index("col")
    ratio = lax.axis_size("row") // lax.axis_size("col")
    current = matrix
    for index in range(PANELS):
        current = reflect(current, index, row_index, column, ratio)
    return current


def solution(mesh):
    in_specs = (P("row", "col"),)
    out_specs = P("row", "col")
    return jax.shard_map(
        per_device, mesh=mesh, in_specs=in_specs, out_specs=out_specs, check_vma=False
    )
```

profile of v0, /device:TPU:1, one launch (start us, length us, event | category | flops | bytes accessed | tf_op | source)
XLA Modules:
  0.0 1592.9 jit_solution(13761343751059832308)
XLA Ops:
  6.5 1.6 copy.8
  8.1 0.9 fusion.3
  9.0 99.1 %all-reduce.16.cloned.1.call-done = f32[512,256]{0,1:T(8,128)} async-done(((f32[512,256]{0,1:T(8,128)}), f32[512,256]{0,1:T(8,128)}) %all-reduce.16.cloned.1.call-update) | async-done | bytes 524304 | tf_op jit(solution)/shard_map/psum | solution.py:15
  108.1 2.5 fusion.90
  110.8 111.6 %all-reduce.18.cloned.1.call-done = f32[256,256]{0,1:T(8,128)} async-done(((f32[256,256]{0,1:T(8,128)}), f32[256,256]{0,1:T(8,128)}) %all-reduce.18.cloned.1.call-update) | async-done | bytes 262160 | tf_op jit(solution)/shard_map/psum | solution.py:49
  222.3 1.1 copy.4
  223.6 11.7 cholesky.214
  235.3 9.8 custom-call.25
  245.6 11.7 cholesky.231
  259.6 15.9 while.16
  272.0 1.4 bitcast_dynamic-update-slice_fusion.8
  274.0 1.4 bitcast_dynamic-update-slice_fusion.8
  275.5 19.7 %custom-call.26 = f32[2,128,128]{1,2,0:T(8,128)S(1)} custom-call(f32[2,128,128]{2,1,0:T(8,128)S(1)} %get-tuple-element.63), custom_call_target="InvertDiagBlocksLowerTriangular" | custom-call | tf_op jit(solution)/shard_map/jit(_solve_triangular)/triangular_solve | solution.py:52
  296.4 0.9 broadcast_select_fusion.2
  297.3 111.3 %all-reduce.20.cloned.1.call-done = f32[512,256]{0,1:T(8,128)} async-done(((f32[512,256]{0,1:T(8,128)}), f32[512,256]{0,1:T(8,128)}) %all-reduce.20.cloned.1.call-update) | async-done | bytes 524304 | tf_op jit(solution)/shard_map/psum | solution.py:15
  408.6 2.9 convolution_bitcast_fusion
  412.3 93.6 %all-reduce.22.cloned.1.call-done = f32[512,256]{0,1:T(8,128)} async-done(((f32[512,256]{0,1:T(8,128)}), f32[512,256]{0,1:T(8,128)}) %all-reduce.22.cloned.1.call-update) | async-done | bytes 524304 | tf_op jit(solution)/shard_map/psum | solution.py:60
  505.9 2.4 fusion.66
  508.4 112.6 %all-reduce.38.cloned.1.call-done = (f32[256,256]{1,0:T(8,128)}, f32[256,256]{1,0:T(8,128)}) async-done(((f32[256,256]{1,0:T(8,128)}, f32[256,256]{1,0:T(8,128)}), (f32[256,256]{1,0:T(8,128)}, f32[256,256]{1,0:T(8,128)})) %all-reduce.38.cloned.1.call-update) | async-done | bytes 524304 | tf_op jit(solution)/shard_map/psum | solution.py:15
  621.0 1.3 fusion.28
  623.8 11.7 cholesky.248
  635.5 9.8 custom-call.28
  645.8 11.7 cholesky.265
  660.2 4.4 while.17
  661.2 1.4 bitcast_dynamic-update-slice_fusion.9
  663.2 1.4 bitcast_dynamic-update-slice_fusion.9
  664.6 19.7 %custom-call.30 = f32[2,128,128]{1,2,0:T(8,128)S(1)} custom-call(f32[2,128,128]{2,1,0:T(8,128)S(1)} %get-tuple-element.66), custom_call_target="InvertDiagBlocksLowerTriangular" | custom-call | tf_op jit(solution)/shard_map/jit(_solve_triangular)/triangular_solve | solution.py:25
  689.0 1.7 broadcast_select_fusion.1
  690.7 1.0 copy-done.6
  691.7 2.1 convolution_subtract_fusion.3
  693.8 108.2 %all-reduce.24.cloned.1.call-done = f32[512,256]{0,1:T(8,128)} async-done(((f32[512,256]{0,1:T(8,128)}), f32[512,256]{0,1:T(8,128)}) %all-reduce.24.cloned.1.call-update) | async-done | bytes 524304 | tf_op jit(solution)/shard_map/psum | solution.py:15
  802.0 2.2 convolution_subtract_fusion.2
  804.2 0.9 fusion.2
  805.1 94.3 %all-reduce.26.cloned.1.call-done = f32[512,256]{0,1:T(8,128)} async-done(((f32[512,256]{0,1:T(8,128)}), f32[512,256]{0,1:T(8,128)}) %all-reduce.26.cloned.1.call-update) | async-done | bytes 524304 | tf_op jit(solution)/shard_map/psum | solution.py:15
  899.4 2.5 fusion.91
  902.2 111.4 %all-reduce.28.cloned.1.call-done = f32[256,256]{0,1:T(8,128)} async-done(((f32[256,256]{0,1:T(8,128)}), f32[256,256]{0,1:T(8,128)}) %all-reduce.28.cloned.1.call-update) | async-done | bytes 262160 | tf_op jit(solution)/shard_map/psum | solution.py:49
  1013.6 1.1 copy.12
  1014.8 11.7 cholesky.282
  1026.6 9.8 custom-call.31
  1036.9 11.7 cholesky.299
  1051.4 4.1 while.18
  1052.0 1.4 bitcast_dynamic-update-slice_fusion.10
  1054.1 1.4 bitcast_dynamic-update-slice_fusion.10
  1055.5 19.7 %custom-call.32 = f32[2,128,128]{1,2,0:T(8,128)S(1)} custom-call(f32[2,128,128]{2,1,0:T(8,128)S(1)} %get-tuple-element.67), custom_call_target="InvertDiagBlocksLowerTriangular" | custom-call | tf_op jit(solution)/shard_map/jit(_solve_triangular)/triangular_solve | solution.py:52
  1076.5 0.9 broadcast_select_fusion.3
  1077.4 111.3 %all-reduce.30.cloned.1.call-done = f32[512,256]{0,1:T(8,128)} async-done(((f32[512,256]{0,1:T(8,128)}), f32[512,256]{0,1:T(8,128)}) %all-reduce.30.cloned.1.call-update) | async-done | bytes 524304 | tf_op jit(solution)/shard_map/psum | solution.py:15
  1188.7 3.6 fusion.92
  1193.2 93.6 %all-reduce.32.cloned.1.call-done = f32[512,256]{1,0:T(8,128)} async-done(((f32[512,256]{1,0:T(8,128)}), f32[512,256]{1,0:T(8,128)}) %all-reduce.32.cloned.1.call-update) | async-done | bytes 524304 | tf_op jit(solution)/shard_map/psum | solution.py:60
  1286.7 2.4 fusion.62
  1289.6 112.2 %all-reduce.36.cloned.1.call-done = (f32[256,256]{1,0:T(8,128)}, f32[256,256]{1,0:T(8,128)}) async-done(((f32[256,256]{1,0:T(8,128)}, f32[256,256]{1,0:T(8,128)}), (f32[256,256]{1,0:T(8,128)}, f32[256,256]{1,0:T(8,128)})) %all-reduce.36.cloned.1.call-update) | async-done | bytes 524304 | tf_op jit(solution)/shard_map/psum | solution.py:15
  1401.9 1.3 fusion.24
  1404.6 11.7 cholesky.316
  1416.3 9.8 custom-call.34
  1426.6 11.7 cholesky.333
  1441.0 4.1 while.19
  1441.8 1.4 bitcast_dynamic-update-slice_fusion.11
  1443.8 1.4 bitcast_dynamic-update-slice_fusion.11
  1445.2 19.7 %custom-call.36 = f32[2,128,128]{1,2,0:T(8,128)S(1)} custom-call(f32[2,128,128]{2,1,0:T(8,128)S(1)} %get-tuple-element.70), custom_call_target="InvertDiagBlocksLowerTriangular" | custom-call | tf_op jit(solution)/shard_map/jit(_solve_triangular)/triangular_solve | solution.py:25
  1469.5 1.7 broadcast_select_fusion
  1471.3 1.0 copy-done.5
  1472.3 2.1 convolution_subtract_fusion.1
  1474.4 108.0 %all-reduce.34.cloned.1.call-done = f32[512,256]{0,1:T(8,128)} async-done(((f32[512,256]{0,1:T(8,128)}), f32[512,256]{0,1:T(8,128)}) %all-reduce.34.cloned.1.call-update) | async-done | bytes 524304 | tf_op jit(solution)/shard_map/psum | solution.py:15
  1582.4 2.2 convolution_subtract_fusion
  1584.6 1.3 copy.18
  (149 shorter events, 29.1 us)
Async XLA Ops:
  6.5 101.6 %all-reduce.16.cloned.1.call-start = ((), (), s32[]{:S(2)}) async-start(), calls=%async_computation | async-start | bytes 1048576 | tf_op jit(solution)/shard_map/psum | solution.py:15
  9.0 213.3 %all-reduce.18.cloned.1.call-start = ((), (), s32[]{:S(2)}) async-start(), calls=%async_computation.1 | async-start | bytes 524288 | tf_op jit(solution)/shard_map/psum | solution.py:49
  110.7 297.9 %all-reduce.20.cloned.1.call-start = ((), (), s32[]{:S(2)}) async-start(), calls=%async_computation.2 | async-start | bytes 1048576 | tf_op jit(solution)/shard_map/psum | solution.py:15
  222.3 1.2 copy-start.7
  259.5 35.7 %copy-start = (f32[512,256]{0,1:T(8,128)S(1)}, f32[512,256]{0,1:T(8,128)}, u32[]{:S(2)}) copy-start(f32[512,256]{0,1:T(8,128)} %all-reduce.16.cloned.1.call-done) | copy-start | bytes 1572868
  296.0 112.7 %copy-start.2 = (f32[512,512]{1,0:T(8,128)S(1)}, f32[512,512]{1,0:T(8,128)}, u32[]{:S(2)}) copy-start(f32[512,512]{1,0:T(8,128)} %param.8) | copy-start | bytes 3145732
  297.3 208.6 %all-reduce.22.cloned.1.call-start = ((), (), s32[]{:S(2)}) async-start(), calls=%async_computation.3 | async-start | bytes 1048576 | tf_op jit(solution)/shard_map/psum | solution.py:60
  411.5 209.5 %all-reduce.38.cloned.1.call-start = ((), (), s32[]{:S(2)}) async-start(), calls=%async_computation.11 | async-start | bytes 1048576 | tf_op jit(solution)/shard_map/psum | solution.py:15
  508.3 293.6 %all-reduce.24.cloned.1.call-start = ((), (), s32[]{:S(2)}) async-start(), calls=%async_computation.4 | async-start | bytes 1048576 | tf_op jit(solution)/shard_map/psum | solution.py:15
  621.0 1.3 copy-start.11
  685.9 1.0 copy-start.10
  687.2 1.0 copy-start.4
  690.7 1.0 copy-start.6
  690.7 208.7 %all-reduce.26.cloned.1.call-start = ((), (), s32[]{:S(2)}) async-start(), calls=%async_computation.5 | async-start | bytes 1048576 | tf_op jit(solution)/shard_map/psum | solution.py:15
  805.0 208.6 %all-reduce.28.cloned.1.call-start = ((), (), s32[]{:S(2)}) async-start(), calls=%async_computation.6 | async-start | bytes 524288 | tf_op jit(solution)/shard_map/psum | solution.py:49
  902.0 286.7 %all-reduce.30.cloned.1.call-start = ((), (), s32[]{:S(2)}) async-start(), calls=%async_computation.7 | async-start | bytes 1048576 | tf_op jit(solution)/shard_map/psum | solution.py:15
  1013.6 1.2 copy-start.8
  1051.4 23.9 %copy-start.1 = (f32[512,256]{0,1:T(8,128)S(1)}, f32[512,256]{0,1:T(8,128)}, u32[]{:S(2)}) copy-start(f32[512,256]{0,1:T(8,128)} %all-reduce.26.cloned.1.call-done) | copy-start | bytes 1572868
  1077.4 209.4 %all-reduce.32.cloned.1.call-start = ((), (), s32[]{:S(2)}) async-start(), calls=%async_computation.8 | async-start | bytes 1048576 | tf_op jit(solution)/shard_map/psum | solution.py:60
  1192.4 209.5 %all-reduce.36.cloned.1.call-start = ((), (), s32[]{:S(2)}) async-start(), calls=%async_computation.10 | async-start | bytes 1048576 | tf_op jit(solution)/shard_map/psum | solution.py:15
  1289.2 293.3 %all-reduce.34.cloned.1.call-start = ((), (), s32[]{:S(2)}) async-start(), calls=%async_computation.9 | async-start | bytes 1048576 | tf_op jit(solution)/shard_map/psum | solution.py:15
  1401.9 1.3 copy-start.12
  1466.5 1.0 copy-start.9
  1467.8 1.0 copy-start.3
  1471.2 1.0 copy-start.5
Sparse Core Ops, SparseCore 0:
  10.5 97.5 all-reduce.15
  110.8 111.4 all-reduce.17
  297.4 111.1 all-reduce.19
  411.7 94.1 all-reduce.21
  508.5 112.5 all-reduce.37
  690.8 111.1 all-reduce.23
  805.2 94.1 all-reduce.25
  902.1 111.4 all-reduce.27
  1077.5 111.1 all-reduce.29
  1192.5 94.1 all-reduce.31
  1289.3 112.5 all-reduce.35
  1471.4 110.9 all-reduce.33
where the time goes:
time: 1600 us; the launch traced here: 1590 us
  waiting for transfers between devices  1270 us (79%)
  other arithmetic  222 us (14%)
  matrix products  44.4 us (3%)
  local copies, waits for them, and re-layouts  25.8 us (2%)
  between operations  19.8 us (1%)
    psum x8, waiting for transfers between devices, broadcast(): return lax.psum(block, axis)  857 us
    psum x2, waiting for transfers between devices, reflect(): gram = lax.psum(local_gram, 'row')  223 us
    psum x2, waiting for transfers between devices, reflect(): product = lax.psum(mult(current, vectors_cols), 'col')  187 us
    another operation x14, other arithmetic, inverse_transposed(): factor = jnp.linalg.cholesky(mult(shifted, shifted.T))  69.2 us
    another operation x13, other arithmetic, reflect(): lower = jnp.linalg.cholesky(gram)  68.7 us
    another operation x5, other arithmetic, reflect(): basis = jax.scipy.linalg.solve_triangular(lower, panel.T, lower=True).T  39.4 us
    another operation x4, other arithmetic, inverse_transposed(): jax.scipy.linalg.solve_triangular(factor, half, lower=True, trans='T')  39.4 us
    dot_general x20, matrix products, mult(): jnp.dot(left, right, precision=HIGH, preferred_element_type=jnp.float32)  32.7 us
  transfers between devices with their start and end apart: 12, of which 12 were waited for; matrix products, arithmetic and copies ran while one was open for 0% of the time, Pallas kernels for 0%

commit v1 on v0

v1 whole, which is shorter than its diff:
```python
import functools

import jax
import jax.numpy as jnp
from jax import lax
from jax.experimental import pallas as pl
from jax.experimental.pallas import tpu as pltpu
from jax.sharding import PartitionSpec as P

BLOCK = 256
PANELS = 2
N = 16
NZ = 8
HIGH = lax.Precision.HIGHEST
F32 = jnp.float32
MESH = pl.DeviceIdType.MESH
VMEM = pl.BlockSpec(memory_space=pltpu.VMEM)


def dot(left, right, over=(1, 0)):
    return lax.dot_general(
        left,
        right,
        (((over[0],), (over[1],)), ((), ())),
        precision=HIGH,
        preferred_element_type=F32,
    )


def sweep(aug, jj, inverse):
    base = pl.multiple_of(8 * jj, 8)
    sub = lax.broadcasted_iota(jnp.int32, (8, 128), 0)
    sub2 = lax.broadcasted_iota(jnp.int32, (8, 256), 0)

    def lane(block, s):
        index = jnp.full((8, 128), base + s, jnp.int32)
        return jnp.take_along_axis(block, index, axis=1)

    group = aug[pl.ds(base, 8), :]
    cols = [lane(group[:, :128], s) for s in range(8)]
    kept = group
    for s in range(8):
        pivot = jnp.broadcast_to(cols[s][s : s + 1], (8, 128))
        inv = 1.0 / pivot
        inv2 = jnp.concatenate([inv, inv], axis=1)
        row = jnp.broadcast_to(group[s : s + 1], (8, 256))
        if not inverse:
            scale = lax.rsqrt(pivot)
            kept = jnp.where(sub2 == s, row * jnp.concatenate([scale, scale], axis=1), kept)
        new = row * inv2
        f = cols[s]
        f2 = jnp.concatenate([f, f], axis=1)
        group = jnp.where(sub2 == s, new, group - f2 * new)
        for t in range(s + 1, 8):
            crow = jnp.broadcast_to(cols[t][s : s + 1], (8, 128)) * inv
            cols[t] = jnp.where(sub == s, crow, cols[t] - f * crow)
    aug[pl.ds(base, 8), :] = group if inverse else kept
    rows = [jnp.broadcast_to(group[s : s + 1], (8, 256)) for s in range(8)]
    for g in range(16):
        block = aug[8 * g : 8 * g + 8, :]
        keep = (g != jj) if inverse else (g > jj)
        new = block
        for s in range(8):
            c = lane(block[:, :128], s)
            new = new - jnp.concatenate([c, c], axis=1) * rows[s]
        aug[8 * g : 8 * g + 8, :] = jnp.where(keep, new, block)


def factor_kernel(t_ref, lt_ref, k_ref, aug):
    eye = (
        lax.broadcasted_iota(jnp.int32, (128, 128), 0)
        == lax.broadcasted_iota(jnp.int32, (128, 128), 1)
    ).astype(F32)
    upper = lax.broadcasted_iota(jnp.int32, (128, 128), 0) <= lax.broadcasted_iota(
        jnp.int32, (128, 128), 1
    )

    def run(block, inverse):
        aug[:, :128] = block
        aug[:, 128:] = eye
        lax.fori_loop(0, 16, lambda jj, _: (sweep(aug, jj, inverse), 0)[1], 0)

    gram = t_ref[0]
    run(gram[:128, :128], False)
    lt00 = jnp.where(upper, aug[:, :128], 0.0)
    lt01 = dot(aug[:, 128:], gram[:128, 128:])
    run(gram[128:, 128:] - dot(lt01, lt01, (0, 0)), False)
    lt_ref[:128, :128] = lt00
    lt_ref[:128, 128:] = lt01
    lt_ref[128:, :128] = jnp.zeros((128, 128), F32)
    lt_ref[128:, 128:] = jnp.where(upper, aug[:, :128], 0.0)
    n = gram + dot(t_ref[1], lt_ref[...], (0, 0))
    run(n[:128, :128], True)
    d0 = aug[:, 128:]
    n01 = dot(d0, n[:128, 128:])
    q = dot(n[128:, :128], d0)
    run(n[128:, 128:] - dot(n[128:, :128], n01), True)
    e = aug[:, 128:]
    k10 = -dot(e, q)
    k_ref[:128, :128] = d0 - dot(n01, k10)
    k_ref[:128, 128:] = -dot(n01, e)
    k_ref[128:, :128] = k10
    k_ref[128:, 128:] = e


def factor(t):
    shape = jax.ShapeDtypeStruct((256, 256), F32)
    return pl.pallas_call(
        factor_kernel,
        out_shape=(shape, shape),
        in_specs=[VMEM],
        out_specs=(VMEM, VMEM),
        scratch_shapes=[pltpu.VMEM((128, 256), F32)],
    )(t)


def remote(src, dst, send, recv, row, col):
    return pltpu.make_async_remote_copy(
        src_ref=src,
        dst_ref=dst,
        send_sem=send,
        recv_sem=recv,
        device_id=(row, col),
        device_id_type=MESH,
    )


def place():
    r, c = lax.axis_index("row"), lax.axis_index("col")
    return r, c, r // 2, lax.rem(r, 2)


def greet(r, c):
    barrier = pltpu.get_barrier_semaphore()
    for k in range(1, N):
        pl.semaphore_signal(barrier, inc=1, device_id=(r, lax.rem(c + k, N)), device_id_type=MESH)
        pl.semaphore_signal(barrier, inc=1, device_id=(lax.rem(r + k, N), c), device_id_type=MESH)
    pl.semaphore_wait(barrier, 2 * (N - 1))


def piece(ref, index, size):
    return ref.at[pl.ds(pl.multiple_of(index * size, size), size)]


SLOT_SEMS = [
    pltpu.SemaphoreType.DMA((2,)),
    pltpu.SemaphoreType.DMA((NZ,)),
    pltpu.SemaphoreType.DMA((NZ,)),
    pltpu.SemaphoreType.DMA((N,)),
    pltpu.SemaphoreType.DMA((N,)),
    pltpu.SemaphoreType.DMA((2,)),
]


def slot_sum(local, pair, ring, out, sems):
    r, c, z, core = place()
    psem, zs, zr, ps, pr, fsem = sems
    mate = r + 1 - 2 * core
    swap = remote(local.at[:, 1 - core], pair, psem.at[0], psem.at[1], mate, c)
    swap.start()
    swap.wait()
    ring[z] = local[:, core] + pair[...]
    across = []
    for k in range(1, NZ):
        zz = lax.rem(z + k, NZ)
        across.append(
            remote(ring.at[z], ring.at[z], zs.at[k], zr.at[z], 2 * zz + core, c)
        )
    for copy in across:
        copy.start()
    for k in range(1, NZ):
        zz = lax.rem(z + k, NZ)
        remote(ring.at[zz], ring.at[zz], zs.at[k], zr.at[zz], r, c).wait_recv()
    total = ring[0]
    for k in range(1, NZ):
        total = total + ring[k]
    out[:, c, core] = total
    around = []
    for k in range(1, N):
        i = lax.rem(c + k, N)
        around.append(
            remote(out.at[:, c, core], out.at[:, c, core], ps.at[k], pr.at[c], r, i)
        )
    for copy in around:
        copy.start()
    for k in range(1, N):
        i = lax.rem(c + k, N)
        remote(out.at[:, i, core], out.at[:, i, core], ps.at[k], pr.at[i], r, c).wait_recv()
    final = remote(out.at[:, :, core], out.at[:, :, core], fsem.at[0], fsem.at[1], mate, c)
    final.start()
    final.wait_send()
    other = 1 - core
    remote(out.at[:, :, other], out.at[:, :, other], fsem.at[0], fsem.at[1], mate, c).wait_recv()
    for copy in across + around:
        copy.wait_send()


def spread_kernel(
    first, lead, a_ref, pr_ref, pct_ref, t_ref, gram, local, pair, ring, s1, r1, s2, s3, r3, s4, s5, *slots
):
    r, c, z, core = place()
    height = a_ref.shape[0]
    root_r, root_c = c == 0, r == 0

    @pl.when(root_r)
    def _():
        rows = r * height + lax.broadcasted_iota(jnp.int32, pr_ref.shape, 0)
        pr_ref[...] = jnp.where(rows >= lead, a_ref[:, first : first + BLOCK], 0.0)

    @pl.when(root_c)
    def _():
        cols = c * height + lax.broadcasted_iota(jnp.int32, pct_ref.shape, 1)
        pct_ref[...] = jnp.where(cols >= lead, a_ref[first : first + BLOCK, :], 0.0)

    greet(r, c)

    def pr_to(p, i, sem):
        return remote(piece(pr_ref, p, 32), piece(pr_ref, p, 32), sem, r1.at[p], r, i)

    def pct_to(p, row, sem):
        return remote(piece(pct_ref, p, 32), piece(pct_ref, p, 32), sem, r3.at[p], row, c)

    root_r_copies = [pr_to(i, i, s1.at[i]) for i in range(1, N)]
    root_r_copies += [pr_to(0, i, s2.at[i]) for i in range(1, N)]
    root_c_copies = [pct_to(p, 2 * p, s3.at[p]) for p in range(1, NZ)]
    root_c_copies += [pct_to(0, 2 * p, s4.at[p]) for p in range(1, NZ)]
    root_c_copies += [pct_to(p, 1, s5.at[p]) for p in range(NZ)]
    ahead_r = []
    for k in range(1, N):
        i = lax.rem(c + k, N)
        ahead_r.append((i, pr_to(c, i, s1.at[k])))
    ahead_c = []
    down_c = [pct_to(z, r + 1, s5.at[0])]
    for k in range(1, NZ):
        zz = lax.rem(z + k, NZ)
        ahead_c.append((zz, pct_to(z, 2 * zz, s3.at[k])))
        down_c.append(pct_to(zz, r + 1, s5.at[k]))

    def got(ref, index, sems):
        remote(piece(ref, index, 32), piece(ref, index, 32), s1.at[0], sems.at[index], r, c).wait_recv()

    @pl.when(root_r)
    def _():
        for copy in root_r_copies:
            copy.start()

    @pl.when(root_c)
    def _():
        for copy in root_c_copies:
            copy.start()

    relay_c = (core == 0) & (z != 0)

    @pl.when(c != 0)
    def _():
        got(pr_ref, c, r1)
        for i, copy in ahead_r:

            @pl.when(i != 0)
            def _():
                copy.start()

    @pl.when(relay_c)
    def _():
        got(pct_ref, z, r3)
        for zz, copy in ahead_c:

            @pl.when(zz != 0)
            def _():
                copy.start()

        down_c[0].start()
        for k in range(1, NZ):
            got(pct_ref, lax.rem(z + k, NZ), r3)
            down_c[k].start()

    @pl.when(core == 1)
    def _():
        for p in range(NZ):
            got(pct_ref, p, r3)

    @pl.when(c != 0)
    def _():
        for k in range(1, N):
            got(pr_ref, lax.rem(c + k, N), r1)

    gram[...] = dot(pr_ref[...], pr_ref[...], (0, 0))
    local[0] = gram[pl.ds(pl.multiple_of(16 * c, 16), 16), :].reshape(2, 8, 256)
    off = lead % height
    top = pr_ref[pl.ds(pl.multiple_of(off + 16 * c, 16), 16), :]
    local[1] = jnp.where(r == lead // height, top, 0.0).reshape(2, 8, 256)
    slot_sum(local, pair, ring, t_ref, slots)

    @pl.when(root_r)
    def _():
        for copy in root_r_copies:
            copy.wait_send()

    @pl.when(root_c)
    def _():
        for copy in root_c_copies:
            copy.wait_send()

    @pl.when(c != 0)
    def _():
        for i, copy in ahead_r:

            @pl.when(i != 0)
            def _():
                copy.wait_send()

    @pl.when(relay_c)
    def _():
        for zz, copy in ahead_c:

            @pl.when(zz != 0)
            def _():
                copy.wait_send()

        for copy in down_c:
            copy.wait_send()


def spread(current, index):
    dma = pltpu.SemaphoreType.DMA
    return pl.pallas_call(
        functools.partial(spread_kernel, index * BLOCK, (index + 1) * BLOCK),
        out_shape=(
            jax.ShapeDtypeStruct((512, 256), F32),
            jax.ShapeDtypeStruct((256, 512), F32),
            jax.ShapeDtypeStruct((2, N, 2, 8, 256), F32),
        ),
        in_specs=[VMEM],
        out_specs=(VMEM,) * 3,
        scratch_shapes=[
            pltpu.VMEM((256, 256), F32),
            pltpu.VMEM((2, 2, 8, 256), F32),
            pltpu.VMEM((2, 8, 256), F32),
            pltpu.VMEM((NZ, 2, 8, 256), F32),
            dma((N,)),
            dma((N,)),
            dma((N,)),
            dma((NZ,)),
            dma((NZ,)),
            dma((NZ,)),
            dma((NZ,)),
        ]
        + SLOT_SEMS,
        compiler_params=pltpu.CompilerParams(collective_id=2 * index, has_side_effects=True),
        name=f"spread{index}",
    )(current)


def gather_kernel(
    wr_ref, wct_ref, m_ref, xr_ref, xct_ref, mt_ref,
    rs_r, rs_m, half, hsum, zbuf, local, pair, ring,
    s1, r1, s2, r2, hs, s3, r3, s4, r4, s5, r5, s6, r6, *slots,
):
    r, c, z, core = place()
    mate = r + 1 - 2 * core
    greet(r, c)
    swap = remote(piece(wct_ref, 1 - core, 128), half, hs.at[0], hs.at[1], mate, c)
    swap.start()
    sends = [swap]
    for k in range(1, N):
        i = lax.rem(c + k, N)
        sends.append(remote(piece(wr_ref, i, 32), rs_r.at[c], s1.at[k], r1.at[c], r, i))
        sends[-1].start()
        sends.append(remote(piece(m_ref, i, 16), rs_m.at[c], s2.at[k], r2.at[c], r, i))
        sends[-1].start()
    rs_r[c] = wr_ref[pl.ds(pl.multiple_of(32 * c, 32), 32), :]
    rs_m[c] = m_ref[pl.ds(pl.multiple_of(16 * c, 16), 16), :]
    swap.wait_recv()
    mine = wct_ref[pl.ds(pl.multiple_of(core * 128, 128), 128), :] + half[...]
    hsum[...] = mine.reshape(NZ, 16, 512)
    zbuf[z] = hsum[z]
    for k in range(1, NZ):
        zz = lax.rem(z + k, NZ)
        sends.append(remote(hsum.at[zz], zbuf.at[z], s3.at[k], r3.at[z], 2 * zz + core, c))
        sends[-1].start()

    def got(ref, sem):
        remote(ref, ref, hs.at[0], sem, r, c).wait_recv()

    for k in range(1, N):
        i = lax.rem(c + k, N)
        got(rs_r.at[i], r1.at[i])
        got(rs_m.at[i], r2.at[i])
    total = rs_r[0]
    total_m = rs_m[0]
    for k in range(1, N):
        total = total + rs_r[k]
        total_m = total_m + rs_m[k]
    xr_ref[pl.ds(pl.multiple_of(32 * c, 32), 32), :] = total
    for k in range(1, N):
        i = lax.rem(c + k, N)
        own = piece(xr_ref, c, 32)
        sends.append(remote(own, own, s4.at[k], r4.at[c], r, i))
        sends[-1].start()
    local[0] = total_m.reshape(2, 8, 256)
    for k in range(1, NZ):
        zz = lax.rem(z + k, NZ)
        got(zbuf.at[zz], r3.at[zz])
    total = zbuf[0]
    for k in range(1, NZ):
        total = total + zbuf[k]
    mine = core * NZ + z
    xct_ref[pl.ds(pl.multiple_of(16 * mine, 16), 16), :] = total
    own = piece(xct_ref, mine, 16)
    for k in range(1, NZ):
        zz = lax.rem(z + k, NZ)
        sends.append(remote(own, own, s5.at[k], r5.at[z], 2 * zz + core, c))
        sends[-1].start()
    sends.append(remote(own, own, s6.at[0], r6.at[z], mate, c))
    sends[-1].start()
    slot_sum(local, pair, ring, mt_ref, slots)
    for k in range(1, NZ):
        zz = lax.rem(z + k, NZ)
        part = piece(xct_ref, core * NZ + zz, 16)
        got(part, r5.at[zz])
        sends.append(remote(part, part, s6.at[k], r6.at[zz], mate, c))
        sends[-1].start()
    for k in range(1, N):
        i = lax.rem(c + k, N)
        got(piece(xr_ref, i, 32), r4.at[i])
    for k in range(NZ):
        got(piece(xct_ref, (1 - core) * NZ + k, 16), r6.at[k])
    for copy in sends:
        copy.wait_send()


def gather(wr, wct, m, index):
    dma = pltpu.SemaphoreType.DMA
    return pl.pallas_call(
        gather_kernel,
        out_shape=(
            jax.ShapeDtypeStruct((512, 256), F32),
            jax.ShapeDtypeStruct((256, 512), F32),
            jax.ShapeDtypeStruct((1, N, 2, 8, 256), F32),
        ),
        in_specs=[VMEM] * 3,
        out_specs=(VMEM,) * 3,
        scratch_shapes=[
            pltpu.VMEM((N, 32, 256), F32),
            pltpu.VMEM((N, 16, 256), F32),
            pltpu.VMEM((128, 512), F32),
            pltpu.VMEM((NZ, 16, 512), F32),
            pltpu.VMEM((NZ, 16, 512), F32),
            pltpu.VMEM((1, 2, 8, 256), F32),
            pltpu.VMEM((1, 8, 256), F32),
            pltpu.VMEM((NZ, 1, 8, 256), F32),
            dma((N,)), dma((N,)), dma((N,)), dma((N,)),
            dma((2,)),
            dma((NZ,)), dma((NZ,)), dma((N,)), dma((N,)),
            dma((NZ,)), dma((NZ,)), dma((NZ,)), dma((NZ,)),
        ]
        + SLOT_SEMS,
        compiler_params=pltpu.CompilerParams(collective_id=2 * index + 1, has_side_effects=True),
        name=f"gather{index}",
    )(wr, wct, m)


def reflect(current, index, row_index, column):
    height = current.shape[0]
    lead = (index + 1) * BLOCK
    owner, off = lead // height, lead % height
    pr, pct, t = spread(current, index)
    lt, k = factor(t.reshape(2, 256, 256))
    low = jnp.pad(lt, ((off, height - off - BLOCK), (0, 0)))
    zr = pr + jnp.where(row_index == owner, low, 0.0)
    zct = pct + jnp.where(column == owner, low.T, 0.0)
    wr = dot(current, zct, (1, 1))
    wct = dot(zr, current, (0, 0))
    m = dot(zr, wr, (0, 0))
    xr, xct, b = gather(wr, wct, m, index)
    half = 0.5 * dot(k, dot(b.reshape(256, 256), k), (0, 0))
    ur = dot(xr, k) - dot(zr, half)
    uct = dot(k, xct, (0, 0)) - dot(half, zct, (0, 0))
    return current - dot(ur, zct) - dot(zr, uct)


def per_device(matrix):
    row_index = lax.axis_index("row")
    column = lax.axis_index("col")
    current = matrix
    for index in range(PANELS):
        current = reflect(current, index, row_index, column)
    return current


def solution(mesh):
    return jax.shard_map(
        per_device, mesh=mesh, in_specs=(P("row", "col"),), out_specs=P("row", "col"), check_vma=False
    )
```

time: 1600 us -> 280 us (0.17)
  waiting for transfers between devices: 1270 us -> 0 us
  Pallas kernels: 0 us -> 246 us
  other arithmetic: 222 us -> 0 us
  local copies, waits for them, and re-layouts: 25.8 us -> 4.53 us
  between operations: 19.8 us -> 0.3 us
  matrix products: 44.4 us -> 28 us
    psum x12 -> x0, waiting for transfers between devices: 1270 us -> none  [the longest x8 857 us: broadcast(): return lax.psum(block, axis)]
    pallas_call x0 -> x6, Pallas kernels: none -> 246 us  [the longest x2 90.6 us: spread(): pl.pallas_call(functools.partial(spread_kernel, index * BLOCK, (index + 1...]
    another operation x36 -> x0, other arithmetic: 217 us -> none  [the longest x14 69.2 us: inverse_transposed(): factor = jnp.linalg.cholesky(mult(shifted, shifted.T))]
    another operation x37 -> x0, local copies, waits for them, and re-layouts: 16.2 us -> none  [the longest x17 8.24 us: reflect(): basis = jax.scipy.linalg.solve_triangular(lower, panel.T, lower=True).T]
    dot_general x20 -> x22, matrix products: 32.7 us -> 28 us  [dot(): lax.dot_general(left, right, (((over[0],), (over[1],)), ((), ())), precis...]
  transfers between devices with their start and end apart: 12 -> 0, of which waited for: 12 -> 0; matrix products, arithmetic and copies ran while one was open for 0% -> 0% of each run, Pallas kernels for 0% -> 0%
where the time goes in v1:
time: 280 us; the launch traced here: 279 us
  Pallas kernels  246 us (88%)
  matrix products  28 us (10%)
  local copies, waits for them, and re-layouts  4.53 us (2%)
    pallas_call x2, Pallas kernels, spread(): pl.pallas_call(functools.partial(spread_kernel, index * BLOCK, (index + 1...  90.6 us
    pallas_call x2, Pallas kernels, factor(): pl.pallas_call(factor_kernel, out_shape=(shape, shape), in_specs=[VMEM],...  82 us
    pallas_call x2, Pallas kernels, gather(): pl.pallas_call(gather_kernel, out_shape=(jax.ShapeDtypeStruct((512, 256),...  73.8 us
    dot_general x22, matrix products, dot(): lax.dot_general(left, right, (((over[0],), (over[1],)), ((), ())), precis...  28 us

profile of v1, /device:TPU:1, one launch (start us, length us, event | category | flops | bytes accessed | tf_op | source)
XLA Modules:
  0.0 279.3 jit_solution(13835744233621854320)
XLA Ops:
  0.0 48.1 %spread0.1 = (f32[512,256]{1,0:T(8,128)}, f32[256,512]{1,0:T(8,128)}, f32[2,16,2,8,256]{4,3,2,1,0:T(8,128)}) custom-call(f32[512,512]{1,0:T(8,128)} %a_ref.1), custom_call_target="tpu_custom_call" | custom-call | tf_op jit(solution)/shard_map/spread0/pallas_call | solution.py:326
  48.1 0.0 copy-start.1
  48.1 1.3 copy.2
  49.4 41.1 %shard_map.17 = (f32[256,256]{1,0:T(8,128)}, f32[256,256]{1,0:T(8,128)}) custom-call(f32[2,256,256]{2,1,0:T(8,128)} %bitcast.54), custom_call_target="tpu_custom_call" | custom-call | tf_op jit(solution)/shard_map/pallas_call | solution.py:108
  90.5 0.0 copy-done.1
  90.5 0.0 copy-start.3
  90.5 0.0 copy-start.4
  90.5 2.9 %fusion.14 = f32[256,512]{1,0:T(8,128)S(1)} fusion(f32[512,512]{1,0:T(8,128)S(1)} %copy-done.1, f32[256,512]{0,1:T(8,128)S(1)} %copy.2, f32[256,256]{1,0:T(8,128)} %get-tuple-element.23, pred[]{:T(512)S(6)} %eq.12), kind=kOutput, calls=%fused_computation.23 | convolution fusion | flops 805568512 | bytes 2359297 | tf_op jit(solution)/shard_map/dot_general | solution.py:21
  93.4 0.0 copy-done.3
  93.5 0.0 copy-done.4
  93.5 1.7 fusion.30.m_ref
  95.2 1.0 copy.3
  96.2 1.9 fusion.32.wct_ref
  98.1 0.0 copy-start.7
  98.1 36.6 %gather0.1 = (f32[512,256]{1,0:T(8,128)}, f32[256,512]{1,0:T(8,128)}, f32[1,16,2,8,256]{4,3,2,1,0:T(8,128)}) custom-call(f32[512,256]{1,0:T(8,128)} %bitcast.53, f32[256,512]{1,0:T(8,128)} %fusion.32.wct_ref, f32[256,256]{1,0:T(8,128)} %fusion.30.m_ref), custom_call_target="tpu_custom_call" | custom-call | tf_op jit(solution)/shard_map/gather0/pallas_call | solution.py:434
  134.6 0.0 copy-done.7
  134.7 0.0 copy-start.11
  134.7 1.7 fusion.34
  136.3 0.0 copy-done.11
  136.3 0.4 fusion.35
  136.7 0.6 convolution_multiply_fusion.1
  137.3 0.6 convolution_subtract_fusion.6
  138.0 0.0 copy-start.9
  138.0 0.6 fusion.11
  138.6 0.4 copy-done.9
  139.0 1.0 fusion
  140.0 1.0 convolution_subtract_fusion.3
  141.1 2.0 convolution_subtract_fusion.2.a_ref
  143.1 42.5 %spread1.1 = (f32[512,256]{1,0:T(8,128)}, f32[256,512]{1,0:T(8,128)}, f32[2,16,2,8,256]{4,3,2,1,0:T(8,128)}) custom-call(f32[512,512]{1,0:T(8,128)} %convolution_subtract_fusion.2.a_ref), custom_call_target="tpu_custom_call" | custom-call | tf_op jit(solution)/shard_map/spread1/pallas_call | solution.py:326
  185.6 0.0 copy-start
  185.6 1.3 copy.4
  186.9 40.9 %shard_map.18 = (f32[256,256]{1,0:T(8,128)}, f32[256,256]{1,0:T(8,128)}) custom-call(f32[2,256,256]{2,1,0:T(8,128)} %bitcast.55), custom_call_target="tpu_custom_call" | custom-call | tf_op jit(solution)/shard_map/pallas_call | solution.py:108
  227.8 0.0 copy-done
  227.8 0.0 copy-start.2
  227.8 0.0 copy-start.5
  227.8 2.0 fusion.9.wr_ref
  229.9 0.0 copy-done.2
  229.9 0.0 copy-done.5
  229.9 0.0 copy-start.6
  229.9 1.7 fusion.24.m_ref
  231.6 0.0 copy-done.6
  231.6 1.9 fusion.26.wct_ref
  233.5 0.0 copy-start.8
  233.5 37.2 %gather1.1 = (f32[512,256]{1,0:T(8,128)}, f32[256,512]{1,0:T(8,128)}, f32[1,16,2,8,256]{4,3,2,1,0:T(8,128)}) custom-call(f32[512,256]{1,0:T(8,128)} %copy-done.6, f32[256,512]{1,0:T(8,128)} %fusion.26.wct_ref, f32[256,256]{1,0:T(8,128)} %fusion.24.m_ref), custom_call_target="tpu_custom_call" | custom-call | tf_op jit(solution)/shard_map/gather1/pallas_call | solution.py:434
  270.8 0.0 copy-done.8
  270.8 0.0 copy-start.12
  270.8 1.7 fusion.36
  272.5 0.0 copy-done.12
  272.5 0.4 fusion.37
  272.9 0.0 copy-start.10
  272.9 0.6 convolution_multiply_fusion
  273.5 0.4 copy-done.10
  273.9 0.6 fusion.38
  274.5 1.1 convolution_subtract_fusion.4
  275.6 0.6 convolution_subtract_fusion.5
  276.2 1.0 convolution_subtract_fusion.1
  277.3 2.0 convolution_subtract_fusion
Async XLA Ops:
  48.1 42.4 %copy-start.1 = (f32[512,512]{1,0:T(8,128)S(1)}, f32[512,512]{1,0:T(8,128)}, u32[]{:S(2)}) copy-start(f32[512,512]{1,0:T(8,128)} %a_ref.1) | copy-start | bytes 3145732
  90.5 2.9 %copy-start.3 = (f32[256,256]{1,0:T(8,128)S(1)}, f32[256,256]{1,0:T(8,128)}, u32[]{:S(2)}) copy-start(f32[256,256]{1,0:T(8,128)} %get-tuple-element.23) | copy-start | bytes 786436
  90.5 2.9 %copy-start.4 = (f32[512,256]{1,0:T(8,128)S(1)}, f32[512,256]{1,0:T(8,128)}, u32[]{:S(2)}) copy-start(f32[512,256]{1,0:T(8,128)} %get-tuple-element.24) | copy-start | bytes 1572868
  98.1 36.6 %copy-start.7 = (f32[256,256]{1,0:T(8,128)S(1)}, f32[256,256]{1,0:T(8,128)}, u32[]{:S(2)}) copy-start(f32[256,256]{1,0:T(8,128)} %get-tuple-element.26) | copy-start | bytes 786436
  134.7 1.7 copy-start.11
  138.0 1.0 copy-start.9
  185.6 42.3 %copy-start = (f32[512,512]{1,0:T(8,128)S(1)}, f32[512,512]{1,0:T(8,128)}, u32[]{:S(2)}) copy-start(f32[512,512]{1,0:T(8,128)} %convolution_subtract_fusion.2.a_ref) | copy-start | bytes 3145732
  227.8 2.0 copy-start.2
  227.8 2.0 copy-start.5
  229.9 1.7 copy-start.6
  233.5 37.2 %copy-start.8 = (f32[256,256]{1,0:T(8,128)S(1)}, f32[256,256]{1,0:T(8,128)}, u32[]{:S(2)}) copy-start(f32[256,256]{1,0:T(8,128)} %get-tuple-element.34) | copy-start | bytes 786436
  270.8 1.7 copy-start.12
  272.9 1.0 copy-start.10

commit v2 on v0

v2 whole, which is shorter than its diff:
```python
import jax
import jax.numpy as jnp
from jax import lax
from jax.experimental import pallas as pl
from jax.experimental.pallas import tpu as pltpu
from jax.sharding import PartitionSpec as P

BLOCK = 256
PANELS = 2
N = 16
NZ = 8
HIGH = lax.Precision.HIGHEST
F32 = jnp.float32
MESH = pl.DeviceIdType.MESH
VMEM = pl.BlockSpec(memory_space=pltpu.VMEM)


def dot(left, right, over=(1, 0)):
    return lax.dot_general(
        left,
        right,
        (((over[0],), (over[1],)), ((), ())),
        precision=HIGH,
        preferred_element_type=F32,
    )


def sweep(aug, jj, inverse):
    base = pl.multiple_of(8 * jj, 8)
    sub = lax.broadcasted_iota(jnp.int32, (8, 128), 0)
    sub2 = lax.broadcasted_iota(jnp.int32, (8, 256), 0)

    def lane(block, s):
        index = jnp.full((8, 128), base + s, jnp.int32)
        return jnp.take_along_axis(block, index, axis=1)

    group = aug[pl.ds(base, 8), :]
    cols = [lane(group[:, :128], s) for s in range(8)]
    kept = group
    for s in range(8):
        pivot = jnp.broadcast_to(cols[s][s : s + 1], (8, 128))
        inv = 1.0 / pivot
        inv2 = jnp.concatenate([inv, inv], axis=1)
        row = jnp.broadcast_to(group[s : s + 1], (8, 256))
        if not inverse:
            scale = lax.rsqrt(pivot)
            kept = jnp.where(sub2 == s, row * jnp.concatenate([scale, scale], axis=1), kept)
        new = row * inv2
        f = cols[s]
        f2 = jnp.concatenate([f, f], axis=1)
        group = jnp.where(sub2 == s, new, group - f2 * new)
        for t in range(s + 1, 8):
            crow = jnp.broadcast_to(cols[t][s : s + 1], (8, 128)) * inv
            cols[t] = jnp.where(sub == s, crow, cols[t] - f * crow)
    aug[pl.ds(base, 8), :] = group if inverse else kept
    rows = [jnp.broadcast_to(group[s : s + 1], (8, 256)) for s in range(8)]
    for g in range(16):
        block = aug[8 * g : 8 * g + 8, :]
        keep = (g != jj) if inverse else (g > jj)
        new = block
        for s in range(8):
            c = lane(block[:, :128], s)
            new = new - jnp.concatenate([c, c], axis=1) * rows[s]
        aug[8 * g : 8 * g + 8, :] = jnp.where(keep, new, block)


def remote(src, dst, send, recv, row, col):
    return pltpu.make_async_remote_copy(
        src_ref=src,
        dst_ref=dst,
        send_sem=send,
        recv_sem=recv,
        device_id=(row, col),
        device_id_type=MESH,
    )


def greet(r, c):
    barrier = pltpu.get_barrier_semaphore()
    for k in range(1, N):
        pl.semaphore_signal(barrier, inc=1, device_id=(r, lax.rem(c + k, N)), device_id_type=MESH)
        pl.semaphore_signal(barrier, inc=1, device_id=(lax.rem(r + k, N), c), device_id_type=MESH)
    pl.semaphore_wait(barrier, 2 * (N - 1))


def at(index, size):
    return pl.ds(pl.multiple_of(index * size, size), size)


def kernel(
    a_ref, out_ref,
    cur, pr, pct, gram, gin, tall, lt_ref, k_ref, n_ref, aug, zr, zct,
    wr, wct, m, inr, inm, half, hsum, zin, xr, xct, mloc, mpair, mring, ball,
    ss, g_r, t_r, p_r, q_r, r_r, m_r, h_r, z_r, x_r, y_r, w_r, s_r, u_r, v_r, f_r,
):
    r, c = lax.axis_index("row"), lax.axis_index("col")
    z, core = r // 2, lax.rem(r, 2)
    mate = r + 1 - 2 * core
    height = a_ref.shape[0]
    eye = (
        lax.broadcasted_iota(jnp.int32, (128, 128), 0)
        == lax.broadcasted_iota(jnp.int32, (128, 128), 1)
    ).astype(F32)
    upper = lax.broadcasted_iota(jnp.int32, (128, 128), 0) <= lax.broadcasted_iota(
        jnp.int32, (128, 128), 1
    )
    plane = [lax.rem(c + k, N) for k in range(1, N)]
    line = [lax.rem(r + k, N) for k in range(1, N)]
    ring = [lax.rem(z + k, NZ) for k in range(1, NZ)]

    def load(block):
        aug[:, :128] = block
        aug[:, 128:] = eye

    def sweeps(lo, hi, inverse):
        lax.fori_loop(lo, hi, lambda jj, _: (sweep(aug, jj, inverse), 0)[1], 0)

    def got(ref, sem):
        remote(ref, ref, ss.at[0], sem, r, c).wait_recv()

    cur[...] = a_ref[...]

    for p in range(PANELS):
        first, lead = p * BLOCK, (p + 1) * BLOCK
        owner, off = lead // height, lead % height
        count = iter(range(1, 400))

        def send(src, dst, sem, row, col):
            return remote(src, dst, ss.at[next(count)], sem, row, col)

        @pl.when(r == 0)
        def _():
            cols = c * height + lax.broadcasted_iota(jnp.int32, (BLOCK, height), 1)
            pct[p] = jnp.where(cols >= lead, cur[first : first + BLOCK, :], 0.0)
            gram[...] = dot(pct[p], pct[p], (1, 1))
            gin[p, c] = gram[at(c, 16), :]

        @pl.when(c == 0)
        def _():
            rows = r * height + lax.broadcasted_iota(jnp.int32, (height, BLOCK), 0)
            pr[p] = jnp.where(rows >= lead, cur[:, first : first + BLOCK], 0.0)

        if p == 0:
            greet(r, c)

        def slot(a, i):
            return tall.at[p, a, i]

        def pr_to(q, i):
            return send(pr.at[p, at(q, 32)], pr.at[p, at(q, 32)], p_r.at[p, q], r, i)

        def pct_to(q, row):
            return send(pct.at[p, at(q, 32)], pct.at[p, at(q, 32)], q_r.at[p, q], row, c)

        g_out = [send(gram.at[at(i, 16)], gin.at[p, c], g_r.at[p, c], r, i) for i in plane]
        top_out = [
            send(pct.at[p, at(i, 16), pl.ds(off, BLOCK)], slot(1, i), t_r.at[p, 1, i], r, i)
            for i in plane
        ]
        down = [send(slot(a, c), slot(a, c), t_r.at[p, a, c], i, c) for a in (0, 1) for i in line]
        share = [
            [send(slot(a, c), slot(a, c), t_r.at[p, a, c], r, i) for i in plane] for a in (0, 1)
        ]
        root_r = [pr_to(i, i) for i in range(1, N)] + [pr_to(0, i) for i in range(1, N)]
        root_c = [pct_to(q, 2 * q) for q in range(1, NZ)] + [pct_to(0, 2 * q) for q in range(1, NZ)]
        root_c += [pct_to(q, 1) for q in range(NZ)]
        ahead_r = [(i, pr_to(c, i)) for i in plane]
        ahead_c = [(q, pct_to(z, 2 * q)) for q in ring]
        low_c = [pct_to(z, r + 1)] + [pct_to(q, r + 1) for q in ring]
        relay = (core == 0) & (z != 0)

        @pl.when(r == 0)
        def _():
            for copy in g_out:
                copy.start()

        @pl.when((r == 0) & (c == owner))
        def _():
            for copy in top_out:
                copy.start()
            tall[p, 1, c] = pct[p, at(c, 16), off : off + BLOCK]

        @pl.when(c == 0)
        def _():
            for copy in root_r:
                copy.start()

        @pl.when(r == 0)
        def _():
            for copy in root_c:
                copy.start()

        @pl.when(c != 0)
        def _():
            got(pr.at[p, at(c, 32)], p_r.at[p, c])
            for i, copy in ahead_r:

                @pl.when(i != 0)
                def _():
                    copy.start()

        @pl.when(r == 0)
        def _():
            for i in plane:
                got(gin.at[p, i], g_r.at[p, i])
            total = gin[p, 0]
            for i in range(1, N):
                total = total + gin[p, i]
            tall[p, 0, c] = total
            for copy in down[: N - 1]:
                copy.start()

            @pl.when(c != owner)
            def _():
                got(slot(1, c), t_r.at[p, 1, c])

            for copy in down[N - 1 :]:
                copy.start()

        @pl.when(relay)
        def _():
            got(pct.at[p, at(z, 32)], q_r.at[p, z])
            for q, copy in ahead_c:

                @pl.when(q != 0)
                def _():
                    copy.start()

            low_c[0].start()

        @pl.when(r != 0)
        def _():
            got(slot(0, c), t_r.at[p, 0, c])

        for copy in share[0]:
            copy.start()

        @pl.when(r != 0)
        def _():
            got(slot(1, c), t_r.at[p, 1, c])

        for copy in share[1]:
            copy.start()

        @pl.when(relay)
        def _():
            for k in range(1, NZ):
                got(pct.at[p, at(ring[k - 1], 32)], q_r.at[p, ring[k - 1]])
                low_c[k].start()

        for i in plane:
            got(slot(0, i), t_r.at[p, 0, i])

        g = tall[p, 0].reshape(BLOCK, BLOCK)
        load(g[:128, :128])
        sweeps(0, 16, False)
        lt00 = jnp.where(upper, aug[:, :128], 0.0)
        lt01 = dot(aug[:, 128:], g[:128, 128:])
        load(g[128:, 128:] - dot(lt01, lt01, (0, 0)))
        sweeps(0, 16, False)
        lt_ref[:128, :128] = lt00
        lt_ref[:128, 128:] = lt01
        lt_ref[128:, :128] = jnp.zeros((128, 128), F32)
        lt_ref[128:, 128:] = jnp.where(upper, aug[:, :128], 0.0)

        @pl.when(core == 1)
        def _():
            for q in range(NZ):
                got(pct.at[p, at(q, 32)], q_r.at[p, q])

        @pl.when(c != 0)
        def _():
            for i in plane:
                got(pr.at[p, at(i, 32)], p_r.at[p, i])

        for i in plane:
            got(slot(1, i), t_r.at[p, 1, i])

        zr[...] = pr[p]
        zct[...] = pct[p]

        @pl.when(r == owner)
        def _():
            zr[off : off + BLOCK, :] = zr[off : off + BLOCK, :] + lt_ref[...]

        @pl.when(c == owner)
        def _():
            zct[:, off : off + BLOCK] = zct[:, off : off + BLOCK] + lt_ref[...].T

        wct[...] = dot(zr[...], cur[...], (0, 0))
        swap = send(wct.at[at(1 - core, 128)], half.at[p], h_r.at[p], mate, c)
        swap.start()
        sends = [swap]

        def go(copy):
            copy.start()
            sends.append(copy)

        wr[...] = dot(cur[...], zct[...], (1, 1))
        for i in plane:
            go(send(wr.at[at(i, 32)], inr.at[p, c], r_r.at[p, c], r, i))
        m[...] = dot(zr[...], wr[...], (0, 0))
        for i in plane:
            go(send(m.at[at(i, 16)], inm.at[p, c], m_r.at[p, c], r, i))
        inr[p, c] = wr[at(c, 32), :]
        inm[p, c] = m[at(c, 16), :]
        swap.wait_recv()
        mine = wct[at(core, 128), :] + half[p]
        hsum[...] = mine.reshape(NZ, 16, 512)
        zin[p, z] = hsum[z]
        for q in ring:
            go(send(hsum.at[q], zin.at[p, z], z_r.at[p, z], 2 * q + core, c))

        n_ref[...] = g + dot(tall[p, 1].reshape(BLOCK, BLOCK), lt_ref[...])
        load(n_ref[:128, :128])
        sweeps(0, 8, True)

        for i in plane:
            got(inr.at[p, i], r_r.at[p, i])
        total = inr[p, 0]
        for i in range(1, N):
            total = total + inr[p, i]
        xr[p, at(c, 32), :] = total
        for i in plane:
            own = xr.at[p, at(c, 32)]
            go(send(own, own, x_r.at[p, c], r, i))
        for i in plane:
            got(inm.at[p, i], m_r.at[p, i])
        total = inm[p, 0]
        for i in range(1, N):
            total = total + inm[p, i]
        mloc[...] = total.reshape(2, 8, BLOCK)
        go(send(mloc.at[1 - core], mpair.at[p], s_r.at[p], mate, c))
        for q in ring:
            got(zin.at[p, q], z_r.at[p, q])
        total = zin[p, 0]
        for q in range(1, NZ):
            total = total + zin[p, q]
        spot = core * NZ + z
        xct[p, at(spot, 16), :] = total
        own = xct.at[p, at(spot, 16)]
        for q in ring:
            go(send(own, own, y_r.at[p, z], 2 * q + core, c))
        go(send(own, own, w_r.at[p, z], mate, c))
        got(mpair.at[p], s_r.at[p])
        mring[p, z] = mloc[core] + mpair[p]
        for q in ring:
            go(send(mring.at[p, z], mring.at[p, z], u_r.at[p, z], 2 * q + core, c))

        sweeps(8, 16, True)
        d0 = aug[:, 128:]
        n01 = dot(d0, n_ref[:128, 128:])
        n10d = dot(n_ref[128:, :128], d0)
        load(n_ref[128:, 128:] - dot(n_ref[128:, :128], n01))

        for q in ring:
            got(mring.at[p, q], u_r.at[p, q])
        total = mring[p, 0]
        for q in range(1, NZ):
            total = total + mring[p, q]
        ball[p, c, core] = total
        own = ball.at[p, c, core]
        for i in plane:
            go(send(own, own, v_r.at[p, c], r, i))
        for q in ring:
            part = xct.at[p, at(core * NZ + q, 16)]
            got(part, y_r.at[p, q])
            go(send(part, part, w_r.at[p, q], mate, c))

        sweeps(0, 8, True)
        for i in plane:
            got(ball.at[p, i, core], v_r.at[p, i])
        final = ball.at[p, :, core]
        go(send(final, final, f_r.at[p], mate, c))
        sweeps(8, 16, True)
        e = aug[:, 128:]
        k10 = -dot(e, n10d)
        k_ref[:128, :128] = d0 - dot(n01, k10)
        k_ref[:128, 128:] = -dot(n01, e)
        k_ref[128:, :128] = k10
        k_ref[128:, 128:] = e

        for i in plane:
            got(xr.at[p, at(i, 32)], x_r.at[p, i])
        for q in range(NZ):
            got(xct.at[p, at((1 - core) * NZ + q, 16)], w_r.at[p, q])
        got(ball.at[p, :, 1 - core], f_r.at[p])

        inner = ball[p].reshape(BLOCK, BLOCK)
        coupled = 0.5 * dot(k_ref[...], dot(inner, k_ref[...]), (0, 0))
        ur = dot(xr[p], k_ref[...]) - dot(zr[...], coupled)
        uct = dot(k_ref[...], xct[p], (0, 0)) - dot(coupled, zct[...], (0, 0))
        dest = out_ref if p == PANELS - 1 else cur
        dest[...] = cur[...] - dot(ur, zct[...]) - dot(zr[...], uct)

        for copy in share[0] + share[1] + sends:
            copy.wait_send()

        @pl.when(r == 0)
        def _():
            for copy in g_out + down + root_c:
                copy.wait_send()

        @pl.when((r == 0) & (c == owner))
        def _():
            for copy in top_out:
                copy.wait_send()

        @pl.when(c == 0)
        def _():
            for copy in root_r:
                copy.wait_send()

        @pl.when(c != 0)
        def _():
            for i, copy in ahead_r:

                @pl.when(i != 0)
                def _():
                    copy.wait_send()

        @pl.when(relay)
        def _():
            for q, copy in ahead_c:

                @pl.when(q != 0)
                def _():
                    copy.wait_send()

            for copy in low_c:
                copy.wait_send()


def per_device(matrix):
    dma = pltpu.SemaphoreType.DMA

    def buf(*shape):
        return pltpu.VMEM(shape, F32)

    return pl.pallas_call(
        kernel,
        out_shape=jax.ShapeDtypeStruct(matrix.shape, F32),
        in_specs=[VMEM],
        out_specs=VMEM,
        scratch_shapes=[
            buf(512, 512),
            buf(2, 512, 256),
            buf(2, 256, 512),
            buf(256, 256),
            buf(2, N, 16, 256),
            buf(2, 2, N, 16, 256),
            buf(256, 256),
            buf(256, 256),
            buf(256, 256),
            buf(128, 256),
            buf(512, 256),
            buf(256, 512),
            buf(512, 256),
            buf(256, 512),
            buf(256, 256),
            buf(2, N, 32, 256),
            buf(2, N, 16, 256),
            buf(2, 128, 512),
            buf(NZ, 16, 512),
            buf(2, NZ, 16, 512),
            buf(2, 512, 256),
            buf(2, 256, 512),
            buf(2, 8, 256),
            buf(2, 8, 256),
            buf(2, NZ, 8, 256),
            buf(2, N, 2, 8, 256),
            dma((400,)),
            dma((2, N)),
            dma((2, 2, N)),
            dma((2, N)),
            dma((2, NZ)),
            dma((2, N)),
            dma((2, N)),
            dma((2,)),
            dma((2, NZ)),
            dma((2, N)),
            dma((2, NZ)),
            dma((2, NZ)),
            dma((2,)),
            dma((2, NZ)),
            dma((2, N)),
            dma((2,)),
        ],
        compiler_params=pltpu.CompilerParams(collective_id=0, has_side_effects=True),
        name="reduce_panels",
    )(matrix)


def solution(mesh):
    return jax.shard_map(
        per_device, mesh=mesh, in_specs=(P("row", "col"),), out_specs=P("row", "col"), check_vma=False
    )
```

time: 1600 us -> 187 us (0.12)
  waiting for transfers between devices: 1270 us -> 0 us
  other arithmetic: 222 us -> 0 us
  Pallas kernels: 0 us -> 183 us
  matrix products: 44.4 us -> 0 us
  local copies, waits for them, and re-layouts: 25.8 us -> 2.26 us
  between operations: 19.8 us -> 0.01 us
    psum x12 -> x0, waiting for transfers between devices: 1270 us -> none  [the longest x8 857 us: broadcast(): return lax.psum(block, axis)]
    another operation x36 -> x0, other arithmetic: 217 us -> none  [the longest x14 69.2 us: inverse_transposed(): factor = jnp.linalg.cholesky(mult(shifted, shifted.T))]
    pallas_call x0 -> x1, Pallas kernels: none -> 183 us  [per_device(): pl.pallas_call(kernel, out_shape=jax.ShapeDtypeStruct(matrix.shape, F32),...]
    dot_general x20 -> x0, matrix products: 32.7 us -> none  [mult(): jnp.dot(left, right, precision=HIGH, preferred_element_type=jnp.float32)]
    another operation x37 -> x0, local copies, waits for them, and re-layouts: 16.2 us -> none  [the longest x17 8.24 us: reflect(): basis = jax.scipy.linalg.solve_triangular(lower, panel.T, lower=True).T]
  transfers between devices with their start and end apart: 12 -> 0, of which waited for: 12 -> 0; matrix products, arithmetic and copies ran while one was open for 0% -> 0% of each run, Pallas kernels for 0% -> 0%
where the time goes in v2:
time: 187 us; the launch traced here: 185 us
  Pallas kernels  183 us (98%)
  local copies, waits for them, and re-layouts  2.26 us (1%)
    pallas_call x1, Pallas kernels, per_device(): pl.pallas_call(kernel, out_shape=jax.ShapeDtypeStruct(matrix.shape, F32),...  183 us

profile of v2, /device:TPU:1, one launch (start us, length us, event | category | flops | bytes accessed | tf_op | source)
XLA Modules:
  0.0 185.0 jit_solution(10127205381783056482)
XLA Ops:
  0.0 182.7 %reduce_panels.1 = f32[512,512]{1,0:T(8,128)} custom-call(f32[512,512]{1,0:T(8,128)} %a_ref.1), custom_call_target="tpu_custom_call" | custom-call | tf_op jit(solution)/shard_map/reduce_panels/pallas_call | solution.py:440
  182.7 2.3 %copy.3 = f32[512,512]{1,0:T(8,128)} copy(f32[512,512]{1,0:T(8,128)} %reduce_panels.1) | data formatting | bytes 2097152

commit v3 on v2

v3 whole, which is shorter than its diff:
```python
import jax
import jax.numpy as jnp
from jax import lax
from jax.experimental import pallas as pl
from jax.experimental.pallas import tpu as pltpu
from jax.sharding import PartitionSpec as P

BLOCK = 256
PANELS = 2
N = 16
NZ = 8
HIGH = lax.Precision.HIGHEST
F32 = jnp.float32
MESH = pl.DeviceIdType.MESH
VMEM = pl.BlockSpec(memory_space=pltpu.VMEM)


def dot(left, right, over=(1, 0)):
    return lax.dot_general(
        left,
        right,
        (((over[0],), (over[1],)), ((), ())),
        precision=HIGH,
        preferred_element_type=F32,
    )


def sweep(aug, jj, inverse):
    base = pl.multiple_of(8 * jj, 8)
    sub = lax.broadcasted_iota(jnp.int32, (8, 128), 0)
    sub2 = lax.broadcasted_iota(jnp.int32, (8, 256), 0)

    def lane(block, s):
        index = jnp.full((8, 128), base + s, jnp.int32)
        return jnp.take_along_axis(block, index, axis=1)

    group = aug[pl.ds(base, 8), :]
    cols = [lane(group[:, :128], s) for s in range(8)]
    kept = group
    for s in range(8):
        pivot = jnp.broadcast_to(cols[s][s : s + 1], (8, 128))
        inv = 1.0 / pivot
        inv2 = jnp.concatenate([inv, inv], axis=1)
        row = jnp.broadcast_to(group[s : s + 1], (8, 256))
        if not inverse:
            scale = lax.rsqrt(pivot)
            kept = jnp.where(sub2 == s, row * jnp.concatenate([scale, scale], axis=1), kept)
        new = row * inv2
        f = cols[s]
        f2 = jnp.concatenate([f, f], axis=1)
        group = jnp.where(sub2 == s, new, group - f2 * new)
        for t in range(s + 1, 8):
            crow = jnp.broadcast_to(cols[t][s : s + 1], (8, 128)) * inv
            cols[t] = jnp.where(sub == s, crow, cols[t] - f * crow)
    aug[pl.ds(base, 8), :] = group if inverse else kept
    rows = [jnp.broadcast_to(group[s : s + 1], (8, 256)) for s in range(8)]
    for g in range(16):
        block = aug[8 * g : 8 * g + 8, :]
        keep = (g != jj) if inverse else (g > jj)
        new = block
        for s in range(8):
            c = lane(block[:, :128], s)
            new = new - jnp.concatenate([c, c], axis=1) * rows[s]
        aug[8 * g : 8 * g + 8, :] = jnp.where(keep, new, block)


def remote(src, dst, send, recv, row, col):
    return pltpu.make_async_remote_copy(
        src_ref=src,
        dst_ref=dst,
        send_sem=send,
        recv_sem=recv,
        device_id=(row, col),
        device_id_type=MESH,
    )


def greet(r, c):
    barrier = pltpu.get_barrier_semaphore()
    for k in range(1, N):
        pl.semaphore_signal(barrier, inc=1, device_id=(r, lax.rem(c + k, N)), device_id_type=MESH)
        pl.semaphore_signal(barrier, inc=1, device_id=(lax.rem(r + k, N), c), device_id_type=MESH)
    pl.semaphore_wait(barrier, 2 * (N - 1))


def at(index, size):
    return pl.ds(pl.multiple_of(index * size, size), size)


def kernel(
    a_ref, out_ref,
    cur, pr, pct, pc, aer, aec, aepr, aepc, gram, gin, tsrc, tall, lt_ref, k_ref, n_ref, aug, zr, zc,
    wr, wc, m, inr, inm, iny, half, hsum, zin, xr, xc, mloc, mpair, mring, ball,
    ss, g_r, b_r, t_r, tm_r, p_r, q_r, ar_r, ac_r, r_r, m_r, yt_r, h_r, z_r, x_r, y_r, w_r, s_r, u_r, v_r, f_r,
):
    r, c = lax.axis_index("row"), lax.axis_index("col")
    z, core = r // 2, lax.rem(r, 2)
    other = 1 - core
    mate = r + 1 - 2 * core
    height = a_ref.shape[0]
    eye = (
        lax.broadcasted_iota(jnp.int32, (128, 128), 0)
        == lax.broadcasted_iota(jnp.int32, (128, 128), 1)
    ).astype(F32)
    upper = lax.broadcasted_iota(jnp.int32, (128, 128), 0) <= lax.broadcasted_iota(
        jnp.int32, (128, 128), 1
    )
    plane = [lax.rem(c + k, N) for k in range(1, N)]
    line = [lax.rem(r + k, N) for k in range(1, N)]
    ring = [lax.rem(z + k, NZ) for k in range(1, NZ)]

    def load(block):
        aug[:, :128] = block
        aug[:, 128:] = eye

    def sweeps(lo, hi, inverse):
        lax.fori_loop(lo, hi, lambda jj, _: (sweep(aug, jj, inverse), 0)[1], 0)

    def got(ref, sem):
        remote(ref, ref, ss.at[0], sem, r, c).wait_recv()

    def when(cond, run):
        pl.when(cond)(run)

    cur[...] = a_ref[...]

    for p in range(PANELS):
        first, lead = p * BLOCK, (p + 1) * BLOCK
        owner, off = lead // height, lead % height
        count = iter(range(1, 480))

        def send(src, dst, sem, row, col):
            return remote(src, dst, ss.at[next(count)], sem, row, col)

        def start(copies):
            for copy in copies:
                copy.start()

        @pl.when(r == 0)
        def _():
            cols = c * height + lax.broadcasted_iota(jnp.int32, (BLOCK, height), 1)
            pct[...] = jnp.where(cols >= lead, cur[first : first + BLOCK, :], 0.0)
            gram[...] = dot(pct[...], pct[...], (1, 1))
            gin[p, c] = gram[at(c, 16), :]

        def slot(a, i, h):
            return tall.at[p, a, i, h]

        def pr_to(q, i):
            return send(pr.at[p, at(q, 32)], pr.at[p, at(q, 32)], p_r.at[p, q], r, i)

        def pc_to(q, row):
            return send(pc.at[p, at(q, 64)], pc.at[p, at(q, 64)], q_r.at[p, q], row, c)

        g_out = [send(gram.at[at(i, 16)], gin.at[p, c], g_r.at[p, c], r, i) for i in plane]
        top_out = [
            send(
                pr.at[p, pl.ds(pl.multiple_of(off + 16 * i + 8 * h, 8), 8)],
                tsrc.at[p, 1, h], b_r.at[p, 1, h], r, i,
            )
            for i in plane for h in (0, 1)
        ]
        ee_out = [
            send(
                aer.at[pl.ds(pl.multiple_of(off + 16 * i + 8 * h, 8), 8)],
                tsrc.at[p, 2, h], b_r.at[p, 2, h], r, i,
            )
            for i in plane for h in (0, 1)
        ]
        down = [
            [
                send(tsrc.at[p, a, lax.rem(i, 2)], slot(a, c, lax.rem(i, 2)), t_r.at[p, a, c, lax.rem(i, 2)], i, c)
                for i in line
            ]
            for a in range(3)
        ]
        share = [
            [send(slot(a, c, core), slot(a, c, core), t_r.at[p, a, c, core], r, i) for i in plane]
            for a in range(3)
        ]
        cross = [
            send(tall.at[p, a, :, core], tall.at[p, a, :, core], tm_r.at[p, a], mate, c)
            for a in range(3)
        ]
        root_r = [pr_to(i, i) for i in range(1, N)] + [pr_to(0, i) for i in range(1, N)]
        root_c = [pc_to(q, 2 * q) for q in range(1, NZ)] + [pc_to(0, 2 * q) for q in range(1, NZ)]
        root_c += [pc_to(q, 1) for q in range(NZ)]
        ae_r = [send(aer.at[at(i, 32)], aepr.at[p], ar_r.at[p], r, i) for i in plane]
        ae_c = [
            send(aec.at[at(lax.rem(i, 2) * NZ + i // 2, 32)], aepc.at[p], ac_r.at[p], i, c)
            for i in line
        ]
        ahead_r = [(i, pr_to(c, i)) for i in plane]
        ahead_c = [(q, pc_to(z, 2 * q)) for q in ring]
        low_c = [pc_to(z, r + 1)] + [pc_to(q, r + 1) for q in ring]
        relay = (core == 0) & (z != 0)

        @pl.when(c == 0)
        def _():
            rows = r * height + lax.broadcasted_iota(jnp.int32, (height, BLOCK), 0)
            pr[p] = jnp.where(rows >= lead, cur[:, first : first + BLOCK], 0.0)

        @pl.when(c == owner)
        def _():
            aer[...] = cur[:, off : off + BLOCK]
            aepr[p] = aer[at(c, 32), :]

        @pl.when(r == owner)
        def _():
            aec[...] = cur[off : off + BLOCK, :].T
            aepc[p] = aec[at(core * NZ + z, 32), :]

        if p == 0:
            greet(r, c)

        when(r == 0, lambda: start(g_out))

        @pl.when((r == owner) & (c == 0))
        def _():
            start(top_out)
            for h in (0, 1):
                tsrc[p, 1, h] = pr[p, pl.ds(pl.multiple_of(off + 16 * c + 8 * h, 8), 8), :]

        when(c == 0, lambda: start(root_r))

        @pl.when(r == 0)
        def _():
            pc[p] = pct[...].T
            start(root_c)

        @pl.when((r == owner) & (c == owner))
        def _():
            start(ee_out)
            for h in (0, 1):
                tsrc[p, 2, h] = aer[pl.ds(pl.multiple_of(off + 16 * c + 8 * h, 8), 8), :]

        @pl.when(r == 0)
        def _():
            for i in plane:
                got(gin.at[p, i], g_r.at[p, i])
            total = gin[p, 0]
            for i in range(1, N):
                total = total + gin[p, i]
            tsrc[p, 0] = total.reshape(2, 8, BLOCK)
            tall[p, 0, c, core] = tsrc[p, 0, core]
            start(down[0])

        @pl.when(c != 0)
        def _():
            got(pr.at[p, at(c, 32)], p_r.at[p, c])
            for i, copy in ahead_r:
                when(i != 0, copy.start)

        @pl.when(relay)
        def _():
            got(pc.at[p, at(z, 64)], q_r.at[p, z])
            for q, copy in ahead_c:
                when(q != 0, copy.start)
            low_c[0].start()

        when(r != 0, lambda: got(slot(0, c, core), t_r.at[p, 0, c, core]))
        start(share[0])

        @pl.when(r == owner)
        def _():
            for a, holder in ((1, 0), (2, owner)):

                @pl.when(c != holder)
                def _():
                    for h in (0, 1):
                        got(tsrc.at[p, a, h], b_r.at[p, a, h])

                tall[p, a, c, core] = tsrc[p, a, core]
                start(down[a])

        when(c == owner, lambda: start(ae_r))
        when(r == owner, lambda: start(ae_c))

        for i in plane:
            got(slot(0, i, core), t_r.at[p, 0, i, core])
        cross[0].start()

        for a in (1, 2):
            when(r != owner, lambda a=a: got(slot(a, c, core), t_r.at[p, a, c, core]))
            start(share[a])

        got(tall.at[p, 0, :, other], tm_r.at[p, 0])

        g = tall[p, 0].reshape(BLOCK, BLOCK)
        load(g[:128, :128])
        sweeps(0, 16, False)
        lt00 = jnp.where(upper, aug[:, :128], 0.0)
        lt01 = dot(aug[:, 128:], g[:128, 128:])
        load(g[128:, 128:] - dot(lt01, lt01, (0, 0)))
        lt_ref[:128, :128] = lt00
        lt_ref[:128, 128:] = lt01
        lt_ref[128:, :128] = jnp.zeros((128, 128), F32)

        @pl.when(relay)
        def _():
            for k in range(1, NZ):
                got(pc.at[p, at(ring[k - 1], 64)], q_r.at[p, ring[k - 1]])
                low_c[k].start()

        @pl.when(c != 0)
        def _():
            for i in plane:
                got(pr.at[p, at(i, 32)], p_r.at[p, i])

        sends = []

        def go(copy):
            copy.start()
            sends.append(copy)

        wc[...] = dot(cur[...], pr[p], (0, 0))
        swap = send(wc.at[at(other, 256)], half.at[p], h_r.at[p], mate, c)
        go(swap)

        @pl.when(core == 1)
        def _():
            for q in range(NZ):
                got(pc.at[p, at(q, 64)], q_r.at[p, q])

        wr[...] = dot(cur[...], pc[p])
        for i in plane:
            go(send(wr.at[at(i, 32)], inr.at[p, c], r_r.at[p, c], r, i))
        inr[p, c] = wr[at(c, 32), :]
        m[...] = dot(pr[p], wr[...], (0, 0))
        for i in plane:
            go(send(m.at[at(i, 16)], inm.at[p, c], m_r.at[p, c], r, i))
        inm[p, c] = m[at(c, 16), :]

        def top_rows(i):
            return pl.ds(pl.multiple_of(off + 16 * i, 16), 16)

        y_out = [send(wr.at[top_rows(i)], iny.at[p, c], yt_r.at[p, c], r, i) for i in plane]

        @pl.when(r == owner)
        def _():
            start(y_out)
            iny[p, c] = wr[top_rows(c), :]

        swap.wait_recv()
        hsum[...] = (wc[at(core, 256), :] + half[p]).reshape(NZ, 32, BLOCK)
        zin[p, z] = hsum[z]
        for q in ring:
            go(send(hsum.at[q], zin.at[p, z], z_r.at[p, z], 2 * q + core, c))

        sweeps(0, 16, False)
        lt_ref[128:, 128:] = jnp.where(upper, aug[:, :128], 0.0)
        lt = lt_ref[...]

        for i in plane:
            got(inr.at[p, i], r_r.at[p, i])
        total = inr[p, 0]
        for i in range(1, N):
            total = total + inr[p, i]
        when(c != owner, lambda: got(aepr.at[p], ar_r.at[p]))
        xr[p, at(c, 32), :] = total + dot(aepr[p], lt)
        for i in plane:
            own = xr.at[p, at(c, 32)]
            go(send(own, own, x_r.at[p, c], r, i))
        for q in ring:
            got(zin.at[p, q], z_r.at[p, q])
        total = zin[p, 0]
        for q in range(1, NZ):
            total = total + zin[p, q]
        when(r != owner, lambda: got(aepc.at[p], ac_r.at[p]))
        spot = core * NZ + z
        xc[p, at(spot, 32), :] = total + dot(aepc[p], lt)
        own = xc.at[p, at(spot, 32)]
        for q in ring:
            go(send(own, own, y_r.at[p, z], 2 * q + core, c))
        go(send(own, own, w_r.at[p, z], mate, c))
        for i in plane:
            got(inm.at[p, i], m_r.at[p, i])
        total = inm[p, 0]
        for i in range(1, N):
            total = total + inm[p, i]
        mloc[0] = total.reshape(2, 8, BLOCK)

        @pl.when(r == owner)
        def _():
            for i in plane:
                got(iny.at[p, i], yt_r.at[p, i])
            total = iny[p, 0]
            for i in range(1, N):
                total = total + iny[p, i]
            mloc[1] = total.reshape(2, 8, BLOCK)

        @pl.when(r != owner)
        def _():
            mloc[1] = jnp.zeros((2, 8, BLOCK), F32)

        go(send(mloc.at[:, other], mpair.at[p], s_r.at[p], mate, c))

        for i in plane:
            got(slot(1, i, core), t_r.at[p, 1, i, core])
        cross[1].start()
        for i in plane:
            got(slot(2, i, core), t_r.at[p, 2, i, core])
        cross[2].start()
        got(mpair.at[p], s_r.at[p])
        mring[p, z] = mloc[:, core] + mpair[p]
        for q in ring:
            go(send(mring.at[p, z], mring.at[p, z], u_r.at[p, z], 2 * q + core, c))
        got(tall.at[p, 1, :, other], tm_r.at[p, 1])
        got(tall.at[p, 2, :, other], tm_r.at[p, 2])

        n_ref[...] = tall[p, 0].reshape(BLOCK, BLOCK) + dot(tall[p, 1].reshape(BLOCK, BLOCK), lt, (0, 0))
        load(n_ref[:128, :128])
        sweeps(0, 16, True)

        for q in ring:
            got(mring.at[p, q], u_r.at[p, q])
        total = mring[p, 0]
        for q in range(1, NZ):
            total = total + mring[p, q]
        ball[p, :, c, core] = total
        own = ball.at[p, :, c, core]
        for i in plane:
            go(send(own, own, v_r.at[p, c], r, i))
        for q in ring:
            part = xc.at[p, at(core * NZ + q, 32)]
            got(part, y_r.at[p, q])
            go(send(part, part, w_r.at[p, q], mate, c))

        d0 = aug[:, 128:]
        n01 = dot(d0, n_ref[:128, 128:])
        n10d = dot(n_ref[128:, :128], d0)
        load(n_ref[128:, 128:] - dot(n_ref[128:, :128], n01))
        sweeps(0, 8, True)
        for i in plane:
            got(ball.at[p, :, i, core], v_r.at[p, i])
        final = ball.at[p, :, :, core]
        go(send(final, final, f_r.at[p], mate, c))
        sweeps(8, 16, True)
        e = aug[:, 128:]
        k10 = -dot(e, n10d)
        k_ref[:128, :128] = d0 - dot(n01, k10)
        k_ref[:128, 128:] = -dot(n01, e)
        k_ref[128:, :128] = k10
        k_ref[128:, 128:] = e

        zr[...] = pr[p]
        zc[...] = pc[p]

        @pl.when(r == owner)
        def _():
            zr[off : off + BLOCK, :] = zr[off : off + BLOCK, :] + lt_ref[...]

        @pl.when(c == owner)
        def _():
            zc[off : off + BLOCK, :] = zc[off : off + BLOCK, :] + lt_ref[...]

        for i in plane:
            got(xr.at[p, at(i, 32)], x_r.at[p, i])
        for q in range(NZ):
            got(xc.at[p, at(other * NZ + q, 32)], w_r.at[p, q])
        got(ball.at[p, :, :, other], f_r.at[p])

        ytop = ball[p, 1].reshape(BLOCK, BLOCK)
        xtop = ytop + dot(tall[p, 2].reshape(BLOCK, BLOCK), lt)
        inner = ball[p, 0].reshape(BLOCK, BLOCK) + dot(ytop, lt, (0, 0)) + dot(lt, xtop, (0, 0))
        coupled = 0.5 * dot(k_ref[...], dot(inner, k_ref[...]), (0, 0))
        ur = dot(xr[p], k_ref[...]) - dot(zr[...], coupled)
        uc = dot(xc[p], k_ref[...]) - dot(zc[...], coupled)
        dest = out_ref if p == PANELS - 1 else cur
        dest[...] = cur[...] - dot(ur, zc[...], (1, 1)) - dot(zr[...], uc, (1, 1))

        def left(copies):
            for copy in copies:
                copy.wait_send()

        left(share[0] + share[1] + share[2] + cross + sends)
        when(r == 0, lambda: left(g_out + down[0] + root_c))
        when(r == owner, lambda: left(down[1] + down[2] + ae_c + y_out))
        when((r == owner) & (c == 0), lambda: left(top_out))
        when((r == owner) & (c == owner), lambda: left(ee_out))
        when(c == 0, lambda: left(root_r))
        when(c == owner, lambda: left(ae_r))

        @pl.when(c != 0)
        def _():
            for i, copy in ahead_r:
                when(i != 0, copy.wait_send)

        @pl.when(relay)
        def _():
            for q, copy in ahead_c:
                when(q != 0, copy.wait_send)
            left(low_c)


def per_device(matrix):
    dma = pltpu.SemaphoreType.DMA

    def buf(*shape):
        return pltpu.VMEM(shape, F32)

    return pl.pallas_call(
        kernel,
        out_shape=jax.ShapeDtypeStruct(matrix.shape, F32),
        in_specs=[VMEM],
        out_specs=VMEM,
        scratch_shapes=[
            buf(512, 512),
            buf(2, 512, 256),
            buf(256, 512),
            buf(2, 512, 256),
            buf(512, 256),
            buf(512, 256),
            buf(2, 32, 256),
            buf(2, 32, 256),
            buf(256, 256),
            buf(2, N, 16, 256),
            buf(2, 3, 2, 8, 256),
            buf(2, 3, N, 2, 8, 256),
            buf(256, 256),
            buf(256, 256),
            buf(256, 256),
            buf(128, 256),
            buf(512, 256),
            buf(512, 256),
            buf(512, 256),
            buf(512, 256),
            buf(256, 256),
            buf(2, N, 32, 256),
            buf(2, N, 16, 256),
            buf(2, N, 16, 256),
            buf(2, 256, 256),
            buf(NZ, 32, 256),
            buf(2, NZ, 32, 256),
            buf(2, 512, 256),
            buf(2, 512, 256),
            buf(2, 2, 8, 256),
            buf(2, 2, 8, 256),
            buf(2, NZ, 2, 8, 256),
            buf(2, 2, N, 2, 8, 256),
            dma((480,)),
            dma((2, N)),
            dma((2, 3, 2)),
            dma((2, 3, N, 2)),
            dma((2, 3)),
            dma((2, N)),
            dma((2, NZ)),
            dma((2,)),
            dma((2,)),
            dma((2, N)),
            dma((2, N)),
            dma((2, N)),
            dma((2,)),
            dma((2, NZ)),
            dma((2, N)),
            dma((2, NZ)),
            dma((2, NZ)),
            dma((2,)),
            dma((2, NZ)),
            dma((2, N)),
            dma((2,)),
        ],
        compiler_params=pltpu.CompilerParams(collective_id=0, has_side_effects=True),
        name="reduce_panels",
    )(matrix)


def solution(mesh):
    return jax.shard_map(
        per_device, mesh=mesh, in_specs=(P("row", "col"),), out_specs=P("row", "col"), check_vma=False
    )
```

time: 187 us -> 182 us (0.973)
  Pallas kernels: 183 us -> 179 us
    pallas_call x1, Pallas kernels: 183 us -> 179 us  [per_device(): pl.pallas_call(kernel, out_shape=jax.ShapeDtypeStruct(matrix.shape, F32),...]
where the time goes in v3:
time: 182 us
  Pallas kernels  179 us (98%)
  local copies, waits for them, and re-layouts  2.26 us (1%)
    pallas_call x1, Pallas kernels, per_device(): pl.pallas_call(kernel, out_shape=jax.ShapeDtypeStruct(matrix.shape, F32),...  179 us

profile of v3, /device:TPU:1, one launch (start us, length us, event | category | flops | bytes accessed | tf_op | source)
XLA Modules:
  0.0 181.5 jit_solution(13488603471767682470)
XLA Ops:
  0.0 179.3 %reduce_panels.1 = f32[512,512]{1,0:T(8,128)} custom-call(f32[512,512]{1,0:T(8,128)} %a_ref.1), custom_call_target="tpu_custom_call" | custom-call | tf_op jit(solution)/shard_map/reduce_panels/pallas_call | solution.py:502
  179.3 2.3 %copy.3 = f32[512,512]{1,0:T(8,128)} copy(f32[512,512]{1,0:T(8,128)} %reduce_panels.1) | data formatting | bytes 2097152

commit v4 on v3

--- a/solution.py
+++ b/solution.py
@@ -25,43 +25,94 @@
     )
 
 
-def sweep(aug, jj, inverse):
-    base = pl.multiple_of(8 * jj, 8)
-    sub = lax.broadcasted_iota(jnp.int32, (8, 128), 0)
-    sub2 = lax.broadcasted_iota(jnp.int32, (8, 256), 0)
-
-    def lane(block, s):
-        index = jnp.full((8, 128), base + s, jnp.int32)
-        return jnp.take_along_axis(block, index, axis=1)
-
-    group = aug[pl.ds(base, 8), :]
-    cols = [lane(group[:, :128], s) for s in range(8)]
-    kept = group
+def recip(x):
+    r = pl.reciprocal(x, approx=True)
+    return r * (2.0 - x * r)
+
+
+def lanes(block, index):
+    return jnp.take_along_axis(block, jnp.full((8, 128), index, jnp.int32), axis=1)
+
+
+def times(scale, row):
+    if row.shape[1] == 128:
+        return scale * row
+    return jnp.concatenate([scale * row[:, :128], scale * row[:, 128:]], axis=1)
+
+
+def put(rows):
+    sub = lax.broadcasted_iota(jnp.int32, rows[0].shape, 0)
+    out = rows[0]
+    for s in range(1, 8):
+        out = jnp.where(sub == s, rows[s], out)
+    return out
+
+
+def group(aug, out, base, inverse):
+    width = aug.shape[1]
+    lane = lax.broadcasted_iota(jnp.int32, (8, 128), 1)
+    inside = (lane >= base) & (lane < base + 8)
+
+    def left(block, value):
+        if width == 128:
+            return jnp.where(inside, value, block)
+        return jnp.concatenate([jnp.where(inside, value, block[:, :128]), block[:, 128:]], axis=1)
+
+    rows = [jnp.broadcast_to(aug[pl.ds(base + s, 1), :], (8, width)) for s in range(8)]
+    e = [[None] * 8 for _ in range(8)]
+    for t in range(8):
+        for s in range(8 if inverse else t + 1):
+            e[s][t] = lanes(rows[s][:, :128], base + t)
+    if inverse:
+        rows = [left(rows[s], (lane == base + s).astype(F32)) for s in range(8)]
+    inv = []
     for s in range(8):
-        pivot = jnp.broadcast_to(cols[s][s : s + 1], (8, 128))
-        inv = 1.0 / pivot
-        inv2 = jnp.concatenate([inv, inv], axis=1)
-        row = jnp.broadcast_to(group[s : s + 1], (8, 256))
-        if not inverse:
-            scale = lax.rsqrt(pivot)
-            kept = jnp.where(sub2 == s, row * jnp.concatenate([scale, scale], axis=1), kept)
-        new = row * inv2
-        f = cols[s]
-        f2 = jnp.concatenate([f, f], axis=1)
-        group = jnp.where(sub2 == s, new, group - f2 * new)
+        inv.append(recip(e[s][s]))
         for t in range(s + 1, 8):
-            crow = jnp.broadcast_to(cols[t][s : s + 1], (8, 128)) * inv
-            cols[t] = jnp.where(sub == s, crow, cols[t] - f * crow)
-    aug[pl.ds(base, 8), :] = group if inverse else kept
-    rows = [jnp.broadcast_to(group[s : s + 1], (8, 256)) for s in range(8)]
-    for g in range(16):
-        block = aug[8 * g : 8 * g + 8, :]
-        keep = (g != jj) if inverse else (g > jj)
-        new = block
-        for s in range(8):
-            c = lane(block[:, :128], s)
-            new = new - jnp.concatenate([c, c], axis=1) * rows[s]
-        aug[8 * g : 8 * g + 8, :] = jnp.where(keep, new, block)
+            f = (e[t][s] if inverse else e[s][t]) * inv[s]
+            for u in range(s + 1 if inverse else t, 8):
+                e[t][u] = e[t][u] - f * e[s][u]
+            rows[t] = rows[t] - times(f, rows[s])
+    if not inverse:
+        out[pl.ds(base, 8), :] = put([times(lax.rsqrt(e[s][s]), rows[s]) for s in range(8)])
+    solved = [None] * 8
+    for s in reversed(range(8)):
+        acc = rows[s]
+        for t in range(s + 1, 8):
+            acc = acc - times(e[s][t], solved[t])
+        solved[s] = times(inv[s], acc)
+    own = put(solved)
+    strip = pl.multiple_of(base // 32 * 32, 32)
+    blocks = [aug[pl.ds(strip + 8 * k, 8), :] for k in range(4)]
+    after = [left(b, 0.0) if inverse else b for b in blocks]
+    for s in range(8):
+        for k in range(4):
+            after[k] = after[k] - times(lanes(blocks[k][:, :128], base + s), solved[s])
+    for k in range(4):
+        aug[pl.ds(strip + 8 * k, 8), :] = jnp.where(strip + 8 * k == base, own, after[k])
+
+
+def strips(aug, out, lo, hi, inverse):
+    row = lax.broadcasted_iota(jnp.int32, (128, 128), 0) // 32
+    lane = lax.broadcasted_iota(jnp.int32, (128, 128), 1) // 32
+
+    def one(k, q):
+        group(aug, out, pl.multiple_of(32 * q + 8 * k, 8), inverse)
+        return q
+
+    def strip(q, carry):
+        lax.fori_loop(0, 4, one, q)
+        aim = (lane == q) & ((row != q) if inverse else (row > q))
+        near = aug[:, :128]
+        prod = dot(jnp.where(aim, near, 0.0), aug[...])
+        if inverse:
+            near = jnp.where(aim, 0.0, near)
+        aug[:, :128] = near - prod[:, :128]
+        if aug.shape[1] > 128:
+            aug[:, 128:] = aug[:, 128:] - prod[:, 128:]
+        return carry
+
+    lax.fori_loop(lo, hi, strip, 0)
 
 
 def remote(src, dst, send, recv, row, col):
@@ -89,7 +140,7 @@
 
 def kernel(
     a_ref, out_ref,
-    cur, pr, pct, pc, aer, aec, aepr, aepc, gram, gin, tsrc, tall, lt_ref, k_ref, n_ref, aug, zr, zc,
+    cur, pr, pct, pc, aer, aec, aepr, aepc, gram, gin, tsrc, tall, lt_ref, k_ref, n_ref, aug, aug2, low, zr, zc,
     wr, wc, m, inr, inm, iny, half, hsum, zin, xr, xc, mloc, mpair, mring, ball,
     ss, g_r, b_r, t_r, tm_r, p_r, q_r, ar_r, ac_r, r_r, m_r, yt_r, h_r, z_r, x_r, y_r, w_r, s_r, u_r, v_r, f_r,
 ):
@@ -98,23 +149,12 @@
     other = 1 - core
     mate = r + 1 - 2 * core
     height = a_ref.shape[0]
-    eye = (
-        lax.broadcasted_iota(jnp.int32, (128, 128), 0)
-        == lax.broadcasted_iota(jnp.int32, (128, 128), 1)
-    ).astype(F32)
     upper = lax.broadcasted_iota(jnp.int32, (128, 128), 0) <= lax.broadcasted_iota(
         jnp.int32, (128, 128), 1
     )
     plane = [lax.rem(c + k, N) for k in range(1, N)]
     line = [lax.rem(r + k, N) for k in range(1, N)]
     ring = [lax.rem(z + k, NZ) for k in range(1, NZ)]
-
-    def load(block):
-        aug[:, :128] = block
-        aug[:, 128:] = eye
-
-    def sweeps(lo, hi, inverse):
-        lax.fori_loop(lo, hi, lambda jj, _: (sweep(aug, jj, inverse), 0)[1], 0)
 
     def got(ref, sem):
         remote(ref, ref, ss.at[0], sem, r, c).wait_recv()
@@ -221,12 +261,7 @@
             for h in (0, 1):
                 tsrc[p, 1, h] = pr[p, pl.ds(pl.multiple_of(off + 16 * c + 8 * h, 8), 8), :]
 
-        when(c == 0, lambda: start(root_r))
-
-        @pl.when(r == 0)
-        def _():
-            pc[p] = pct[...].T
-            start(root_c)
+        when((c == 0) & (r > 1), lambda: start(root_r))
 
         @pl.when((r == owner) & (c == owner))
         def _():
@@ -245,6 +280,15 @@
             tall[p, 0, c, core] = tsrc[p, 0, core]
             start(down[0])
 
+        when(r != 0, lambda: got(slot(0, c, core), t_r.at[p, 0, c, core]))
+        start(share[0])
+        when((c == 0) & (r <= 1), lambda: start(root_r))
+
+        @pl.when(r == 0)
+        def _():
+            pc[p] = pct[...].T
+            start(root_c)
+
         @pl.when(c != 0)
         def _():
             got(pr.at[p, at(c, 32)], p_r.at[p, c])
@@ -258,8 +302,6 @@
                 when(q != 0, copy.start)
             low_c[0].start()
 
-        when(r != 0, lambda: got(slot(0, c, core), t_r.at[p, 0, c, core]))
-        start(share[0])
 
         @pl.when(r == owner)
         def _():
@@ -273,9 +315,6 @@
                 tall[p, a, c, core] = tsrc[p, a, core]
                 start(down[a])
 
-        when(c == owner, lambda: start(ae_r))
-        when(r == owner, lambda: start(ae_c))
-
         for i in plane:
             got(slot(0, i, core), t_r.at[p, 0, i, core])
         cross[0].start()
@@ -286,14 +325,15 @@
 
         got(tall.at[p, 0, :, other], tm_r.at[p, 0])
 
+        when(c == owner, lambda: start(ae_r))
+        when(r == owner, lambda: start(ae_c))
+
         g = tall[p, 0].reshape(BLOCK, BLOCK)
-        load(g[:128, :128])
-        sweeps(0, 16, False)
-        lt00 = jnp.where(upper, aug[:, :128], 0.0)
-        lt01 = dot(aug[:, 128:], g[:128, 128:])
-        load(g[128:, 128:] - dot(lt01, lt01, (0, 0)))
-        lt_ref[:128, :128] = lt00
-        lt_ref[:128, 128:] = lt01
+        aug[...] = g[:128, :]
+        strips(aug, lt_ref, 0, 4, False)
+        lt_ref[:128, :128] = jnp.where(upper, lt_ref[:128, :128], 0.0)
+        lt01 = lt_ref[:128, 128:]
+        aug2[...] = g[128:, 128:] - dot(lt01, lt01, (0, 0))
         lt_ref[128:, :128] = jnp.zeros((128, 128), F32)
 
         @pl.when(relay)
@@ -347,8 +387,8 @@
         for q in ring:
             go(send(hsum.at[q], zin.at[p, z], z_r.at[p, z], 2 * q + core, c))
 
-        sweeps(0, 16, False)
-        lt_ref[128:, 128:] = jnp.where(upper, aug[:, :128], 0.0)
+        strips(aug2, low, 0, 4, False)
+        lt_ref[128:, 128:] = jnp.where(upper, low[...], 0.0)
         lt = lt_ref[...]
 
         for i in plane:
@@ -409,8 +449,8 @@
         got(tall.at[p, 2, :, other], tm_r.at[p, 2])
 
         n_ref[...] = tall[p, 0].reshape(BLOCK, BLOCK) + dot(tall[p, 1].reshape(BLOCK, BLOCK), lt, (0, 0))
-        load(n_ref[:128, :128])
-        sweeps(0, 16, True)
+        aug[...] = n_ref[:128, :]
+        strips(aug, None, 0, 4, True)
 
         for q in ring:
             got(mring.at[p, q], u_r.at[p, q])
@@ -426,17 +466,17 @@
             got(part, y_r.at[p, q])
             go(send(part, part, w_r.at[p, q], mate, c))
 
-        d0 = aug[:, 128:]
-        n01 = dot(d0, n_ref[:128, 128:])
+        d0 = aug[:, :128]
+        n01 = aug[:, 128:]
         n10d = dot(n_ref[128:, :128], d0)
-        load(n_ref[128:, 128:] - dot(n_ref[128:, :128], n01))
-        sweeps(0, 8, True)
+        aug2[...] = n_ref[128:, 128:] - dot(n_ref[128:, :128], n01)
+        strips(aug2, None, 0, 2, True)
         for i in plane:
             got(ball.at[p, :, i, core], v_r.at[p, i])
         final = ball.at[p, :, :, core]
         go(send(final, final, f_r.at[p], mate, c))
-        sweeps(8, 16, True)
-        e = aug[:, 128:]
+        strips(aug2, None, 2, 4, True)
+        e = aug2[...]
         k10 = -dot(e, n10d)
         k_ref[:128, :128] = d0 - dot(n01, k10)
         k_ref[:128, 128:] = -dot(n01, e)
@@ -521,6 +561,8 @@
             buf(256, 256),
             buf(256, 256),
             buf(128, 256),
+            buf(128, 128),
+            buf(128, 128),
             buf(512, 256),
             buf(512, 256),
             buf(512, 256),

time: 182 us -> 159 us (0.87)
  Pallas kernels: 179 us -> 156 us
    pallas_call x1, Pallas kernels: 179 us -> 156 us  [per_device(): pl.pallas_call(kernel, out_shape=jax.ShapeDtypeStruct(matrix.shape, F32),...]
where the time goes in v4:
time: 159 us; the launch traced here: 158 us
  Pallas kernels  156 us (98%)
  local copies, waits for them, and re-layouts  2.26 us (1%)
    pallas_call x1, Pallas kernels, per_device(): pl.pallas_call(kernel, out_shape=jax.ShapeDtypeStruct(matrix.shape, F32),...  156 us

profile of v4, /device:TPU:1, one launch (start us, length us, event | category | flops | bytes accessed | tf_op | source)
XLA Modules:
  0.0 158.5 jit_solution(16824566121315928095)
XLA Ops:
  0.0 156.2 %reduce_panels.1 = f32[512,512]{1,0:T(8,128)} custom-call(f32[512,512]{1,0:T(8,128)} %a_ref.1), custom_call_target="tpu_custom_call" | custom-call | tf_op jit(solution)/shard_map/reduce_panels/pallas_call | solution.py:542
  156.2 2.3 %copy.3 = f32[512,512]{1,0:T(8,128)} copy(f32[512,512]{1,0:T(8,128)} %reduce_panels.1) | data formatting | bytes 2097152

commit v5 on v4

--- a/solution.py
+++ b/solution.py
@@ -140,9 +140,10 @@
 
 def kernel(
     a_ref, out_ref,
-    cur, pr, pct, pc, aer, aec, aepr, aepc, gram, gin, tsrc, tall, lt_ref, k_ref, n_ref, aug, aug2, low, zr, zc,
-    wr, wc, m, inr, inm, iny, half, hsum, zin, xr, xc, mloc, mpair, mring, ball,
-    ss, g_r, b_r, t_r, tm_r, p_r, q_r, ar_r, ac_r, r_r, m_r, yt_r, h_r, z_r, x_r, y_r, w_r, s_r, u_r, v_r, f_r,
+    cur, pr, pct, pc, aer, aec, aepr, aepc, aefr, aefc, gram, gin, tsrc, tall, lt_ref, k_ref, n_ref, aug, aug2, low,
+    zr, zc, wr, wc, m, mpair, mh, ybuf, yin, inr, inm, iny, half, hsum, zin, xr, xc, mring, ball,
+    ss, g_r, b_r, t_r, tm_r, p_r, q_r, ar_r, ac_r, af_r, ag_r, am_r,
+    r_r, m_r, yt_r, ys_r, h_r, z_r, x_r, y_r, w_r, s_r, u_r, v_r, f_r,
 ):
     r, c = lax.axis_index("row"), lax.axis_index("col")
     z, core = r // 2, lax.rem(r, 2)
@@ -163,11 +164,13 @@
         pl.when(cond)(run)
 
     cur[...] = a_ref[...]
+    zown = 0
 
     for p in range(PANELS):
         first, lead = p * BLOCK, (p + 1) * BLOCK
         owner, off = lead // height, lead % height
         count = iter(range(1, 480))
+        sends = []
 
         def send(src, dst, sem, row, col):
             return remote(src, dst, ss.at[next(count)], sem, row, col)
@@ -176,21 +179,47 @@
             for copy in copies:
                 copy.start()
 
-        @pl.when(r == 0)
-        def _():
-            cols = c * height + lax.broadcasted_iota(jnp.int32, (BLOCK, height), 1)
-            pct[...] = jnp.where(cols >= lead, cur[first : first + BLOCK, :], 0.0)
-            gram[...] = dot(pct[...], pct[...], (1, 1))
-            gin[p, c] = gram[at(c, 16), :]
+        def go(copy):
+            copy.start()
+            sends.append(copy)
 
         def slot(a, i, h):
             return tall.at[p, a, i, h]
 
         def pr_to(q, i):
-            return send(pr.at[p, at(q, 32)], pr.at[p, at(q, 32)], p_r.at[p, q], r, i)
+            return send(pr.at[p, at(q, 32)], pr.at[p, at(q, 32)], p_r.at[q], r, i)
 
         def pc_to(q, row):
-            return send(pc.at[p, at(q, 64)], pc.at[p, at(q, 64)], q_r.at[p, q], row, c)
+            return send(pc.at[p, at(q, 64)], pc.at[p, at(q, 64)], q_r.at[q], row, c)
+
+        def aer_at(i):
+            return aefr.at[at(i, 32)] if p == 0 else aepr
+
+        def aec_at(i):
+            return aefc.at[at(i, 32)] if p == 0 else aepc
+
+        spot = core * NZ + z
+
+        if p == 0:
+
+            @pl.when(r == 0)
+            def _():
+                cols = c * height + lax.broadcasted_iota(jnp.int32, (BLOCK, height), 1)
+                pct[...] = jnp.where(cols >= lead, cur[first : first + BLOCK, :], 0.0)
+                gram[...] = dot(pct[...], pct[...], (1, 1))
+                gin[p, c] = gram[at(c, 16), :]
+
+            @pl.when(c == 0)
+            def _():
+                rows = r * height + lax.broadcasted_iota(jnp.int32, (height, BLOCK), 0)
+                pr[p] = jnp.where(rows >= lead, cur[:, first : first + BLOCK], 0.0)
+
+        else:
+
+            @pl.when(r == 0)
+            def _():
+                gram[...] = dot(pc[p], pc[p], (0, 0))
+                gin[p, c] = gram[at(c, 16), :]
 
         g_out = [send(gram.at[at(i, 16)], gin.at[p, c], g_r.at[p, c], r, i) for i in plane]
         top_out = [
@@ -222,33 +251,37 @@
             send(tall.at[p, a, :, core], tall.at[p, a, :, core], tm_r.at[p, a], mate, c)
             for a in range(3)
         ]
-        root_r = [pr_to(i, i) for i in range(1, N)] + [pr_to(0, i) for i in range(1, N)]
-        root_c = [pc_to(q, 2 * q) for q in range(1, NZ)] + [pc_to(0, 2 * q) for q in range(1, NZ)]
-        root_c += [pc_to(q, 1) for q in range(NZ)]
-        ae_r = [send(aer.at[at(i, 32)], aepr.at[p], ar_r.at[p], r, i) for i in plane]
+        ae_r = [send(aer.at[at(i, 32)], aer_at(i), ar_r.at[p], r, i) for i in plane]
         ae_c = [
-            send(aec.at[at(lax.rem(i, 2) * NZ + i // 2, 32)], aepc.at[p], ac_r.at[p], i, c)
+            send(aec.at[at(lax.rem(i, 2) * NZ + i // 2, 32)], aec_at(lax.rem(i, 2) * NZ + i // 2), ac_r.at[p], i, c)
             for i in line
         ]
-        ahead_r = [(i, pr_to(c, i)) for i in plane]
-        ahead_c = [(q, pc_to(z, 2 * q)) for q in ring]
-        low_c = [pc_to(z, r + 1)] + [pc_to(q, r + 1) for q in ring]
         relay = (core == 0) & (z != 0)
-
-        @pl.when(c == 0)
-        def _():
-            rows = r * height + lax.broadcasted_iota(jnp.int32, (height, BLOCK), 0)
-            pr[p] = jnp.where(rows >= lead, cur[:, first : first + BLOCK], 0.0)
+        if p == 0:
+            root_r = [pr_to(i, i) for i in range(1, N)] + [pr_to(0, i) for i in range(1, N)]
+            root_c = [pc_to(q, 2 * q) for q in range(1, NZ)] + [pc_to(0, 2 * q) for q in range(1, NZ)]
+            root_c += [pc_to(q, 1) for q in range(NZ)]
+            ahead_r = [(i, pr_to(c, i)) for i in plane]
+            ahead_c = [(q, pc_to(z, 2 * q)) for q in ring]
+            low_c = [pc_to(z, r + 1)] + [pc_to(q, r + 1) for q in ring]
 
         @pl.when(c == owner)
         def _():
             aer[...] = cur[:, off : off + BLOCK]
-            aepr[p] = aer[at(c, 32), :]
+            mine = aer[at(c, 32), :]
+            if p == 0:
+                aefr[at(c, 32), :] = mine
+            else:
+                aepr[...] = mine
 
         @pl.when(r == owner)
         def _():
             aec[...] = cur[off : off + BLOCK, :].T
-            aepc[p] = aec[at(core * NZ + z, 32), :]
+            mine = aec[at(spot, 32), :]
+            if p == 0:
+                aefc[at(spot, 32), :] = mine
+            else:
+                aepc[...] = mine
 
         if p == 0:
             greet(r, c)
@@ -261,13 +294,63 @@
             for h in (0, 1):
                 tsrc[p, 1, h] = pr[p, pl.ds(pl.multiple_of(off + 16 * c + 8 * h, 8), 8), :]
 
-        when((c == 0) & (r > 1), lambda: start(root_r))
+        if p == 0:
+            when((c == 0) & (r > 1), lambda: start(root_r))
 
         @pl.when((r == owner) & (c == owner))
         def _():
             start(ee_out)
             for h in (0, 1):
                 tsrc[p, 2, h] = aer[pl.ds(pl.multiple_of(off + 16 * c + 8 * h, 8), 8), :]
+
+        swap = send(wc.at[at(other, 256)], half.at[p], h_r.at[p], mate, c)
+        mswap = send(m.at[:, other], mpair.at[p], s_r.at[p], mate, c)
+        yswap = send(ybuf.at[:, other], yin.at[p], ys_r.at[p], mate, c)
+        y_own = [send(ybuf.at[i, core], iny.at[p, c], yt_r.at[p, c], r, i) for i in plane]
+        y_mate = [send(yin.at[p, i], iny.at[p, c], yt_r.at[p, c], r, i) for i in plane]
+
+        def products():
+            wc[...] = dot(cur[...], pr[p], (0, 0))
+            go(swap)
+            wr[...] = dot(cur[...], pc[p])
+
+            @pl.when(r == owner)
+            def _():
+                ybuf[...] = wr[off : off + BLOCK, :].reshape(N, 2, 8, BLOCK)
+                yswap.start()
+
+            m[...] = dot(pr[p], wr[...], (0, 0)).reshape(N, 2, 8, BLOCK)
+            go(mswap)
+
+        def scatter():
+            mswap.wait_recv()
+            mh[...] = m[:, core] + mpair[p]
+            for i in plane:
+                go(send(mh.at[i], inm.at[p, c], m_r.at[p, c], r, i))
+            inm[p, c] = mh[c]
+
+            @pl.when(r == owner)
+            def _():
+                start(y_own)
+                iny[p, c] = ybuf[c, core]
+
+            @pl.when(mate == owner)
+            def _():
+                yswap.wait_recv()
+                start(y_mate)
+                iny[p, c] = yin[p, c]
+
+            for i in plane:
+                go(send(wr.at[at(i, 32)], inr.at[p, c], r_r.at[p, c], r, i))
+            inr[p, c] = wr[at(c, 32), :]
+            swap.wait_recv()
+            hsum[...] = (wc[at(core, 256), :] + half[p]).reshape(NZ, 32, BLOCK)
+            zin[p, z] = hsum[z]
+            for q in ring:
+                go(send(hsum.at[q], zin.at[p, z], z_r.at[p, z], 2 * q + core, c))
+
+        if p > 0:
+            products()
 
         @pl.when(r == 0)
         def _():
@@ -282,26 +365,21 @@
 
         when(r != 0, lambda: got(slot(0, c, core), t_r.at[p, 0, c, core]))
         start(share[0])
-        when((c == 0) & (r <= 1), lambda: start(root_r))
-
-        @pl.when(r == 0)
-        def _():
-            pc[p] = pct[...].T
-            start(root_c)
-
-        @pl.when(c != 0)
-        def _():
-            got(pr.at[p, at(c, 32)], p_r.at[p, c])
-            for i, copy in ahead_r:
-                when(i != 0, copy.start)
-
-        @pl.when(relay)
-        def _():
-            got(pc.at[p, at(z, 64)], q_r.at[p, z])
-            for q, copy in ahead_c:
-                when(q != 0, copy.start)
-            low_c[0].start()
-
+
+        if p == 0:
+            when((c == 0) & (r <= 1), lambda: start(root_r))
+
+            @pl.when(r == 0)
+            def _():
+                pc[p] = pct[...].T
+                start(root_c)
+
+            @pl.when(relay)
+            def _():
+                got(pc.at[p, at(z, 64)], q_r.at[z])
+                for q, copy in ahead_c:
+                    when(q != 0, copy.start)
+                low_c[0].start()
 
         @pl.when(r == owner)
         def _():
@@ -319,14 +397,24 @@
             got(slot(0, i, core), t_r.at[p, 0, i, core])
         cross[0].start()
 
+        if p == 0:
+
+            @pl.when(c != 0)
+            def _():
+                got(pr.at[p, at(c, 32)], p_r.at[c])
+                for i, copy in ahead_r:
+                    when(i != 0, copy.start)
+
+        else:
+            scatter()
+
         for a in (1, 2):
             when(r != owner, lambda a=a: got(slot(a, c, core), t_r.at[p, a, c, core]))
             start(share[a])
 
-        got(tall.at[p, 0, :, other], tm_r.at[p, 0])
-
         when(c == owner, lambda: start(ae_r))
         when(r == owner, lambda: start(ae_c))
+        got(tall.at[p, 0, :, other], tm_r.at[p, 0])
 
         g = tall[p, 0].reshape(BLOCK, BLOCK)
         aug[...] = g[:128, :]
@@ -336,121 +424,109 @@
         aug2[...] = g[128:, 128:] - dot(lt01, lt01, (0, 0))
         lt_ref[128:, :128] = jnp.zeros((128, 128), F32)
 
-        @pl.when(relay)
-        def _():
-            for k in range(1, NZ):
-                got(pc.at[p, at(ring[k - 1], 64)], q_r.at[p, ring[k - 1]])
-                low_c[k].start()
-
-        @pl.when(c != 0)
-        def _():
+        if p == 0:
+
+            @pl.when(relay)
+            def _():
+                for k in range(1, NZ):
+                    got(pc.at[p, at(ring[k - 1], 64)], q_r.at[ring[k - 1]])
+                    low_c[k].start()
+
+            @pl.when(c != 0)
+            def _():
+                for i in plane:
+                    got(pr.at[p, at(i, 32)], p_r.at[i])
+
+            @pl.when(core == 1)
+            def _():
+                for q in range(NZ):
+                    got(pc.at[p, at(q, 64)], q_r.at[q])
+
+            products()
+            scatter()
+
+        for a in (1, 2):
             for i in plane:
-                got(pr.at[p, at(i, 32)], p_r.at[p, i])
-
-        sends = []
-
-        def go(copy):
-            copy.start()
-            sends.append(copy)
-
-        wc[...] = dot(cur[...], pr[p], (0, 0))
-        swap = send(wc.at[at(other, 256)], half.at[p], h_r.at[p], mate, c)
-        go(swap)
-
-        @pl.when(core == 1)
-        def _():
-            for q in range(NZ):
-                got(pc.at[p, at(q, 64)], q_r.at[p, q])
-
-        wr[...] = dot(cur[...], pc[p])
-        for i in plane:
-            go(send(wr.at[at(i, 32)], inr.at[p, c], r_r.at[p, c], r, i))
-        inr[p, c] = wr[at(c, 32), :]
-        m[...] = dot(pr[p], wr[...], (0, 0))
-        for i in plane:
-            go(send(m.at[at(i, 16)], inm.at[p, c], m_r.at[p, c], r, i))
-        inm[p, c] = m[at(c, 16), :]
-
-        def top_rows(i):
-            return pl.ds(pl.multiple_of(off + 16 * i, 16), 16)
-
-        y_out = [send(wr.at[top_rows(i)], iny.at[p, c], yt_r.at[p, c], r, i) for i in plane]
-
-        @pl.when(r == owner)
-        def _():
-            start(y_out)
-            iny[p, c] = wr[top_rows(c), :]
-
-        swap.wait_recv()
-        hsum[...] = (wc[at(core, 256), :] + half[p]).reshape(NZ, 32, BLOCK)
-        zin[p, z] = hsum[z]
-        for q in ring:
-            go(send(hsum.at[q], zin.at[p, z], z_r.at[p, z], 2 * q + core, c))
+                got(slot(a, i, core), t_r.at[p, a, i, core])
+            cross[a].start()
 
         strips(aug2, low, 0, 4, False)
         lt_ref[128:, 128:] = jnp.where(upper, low[...], 0.0)
         lt = lt_ref[...]
 
-        for i in plane:
-            got(inr.at[p, i], r_r.at[p, i])
-        total = inr[p, 0]
-        for i in range(1, N):
-            total = total + inr[p, i]
-        when(c != owner, lambda: got(aepr.at[p], ar_r.at[p]))
-        xr[p, at(c, 32), :] = total + dot(aepr[p], lt)
-        for i in plane:
+        def sums():
+            for i in plane:
+                got(inm.at[p, i], m_r.at[p, i])
+            total = inm[p, 0]
+            for i in range(1, N):
+                total = total + inm[p, i]
+            mring[p, z, 0] = total
+
+            @pl.when(z == zown)
+            def _():
+                for i in plane:
+                    got(iny.at[p, i], yt_r.at[p, i])
+                total = iny[p, 0]
+                for i in range(1, N):
+                    total = total + iny[p, i]
+                mring[p, z, 1] = total
+
+            @pl.when(z != zown)
+            def _():
+                mring[p, z, 1] = jnp.zeros((8, BLOCK), F32)
+
+            for q in ring:
+                go(send(mring.at[p, z], mring.at[p, z], u_r.at[p, z], 2 * q + core, c))
+            for i in plane:
+                got(inr.at[p, i], r_r.at[p, i])
+            total = inr[p, 0]
+            for i in range(1, N):
+                total = total + inr[p, i]
+            mine = aer_at(c)
+            when(c != owner, lambda: got(mine, ar_r.at[p]))
+            xr[p, at(c, 32), :] = total + dot(mine[...], lt)
             own = xr.at[p, at(c, 32)]
-            go(send(own, own, x_r.at[p, c], r, i))
-        for q in ring:
-            got(zin.at[p, q], z_r.at[p, q])
-        total = zin[p, 0]
-        for q in range(1, NZ):
-            total = total + zin[p, q]
-        when(r != owner, lambda: got(aepc.at[p], ac_r.at[p]))
-        spot = core * NZ + z
-        xc[p, at(spot, 32), :] = total + dot(aepc[p], lt)
-        own = xc.at[p, at(spot, 32)]
-        for q in ring:
-            go(send(own, own, y_r.at[p, z], 2 * q + core, c))
-        go(send(own, own, w_r.at[p, z], mate, c))
-        for i in plane:
-            got(inm.at[p, i], m_r.at[p, i])
-        total = inm[p, 0]
-        for i in range(1, N):
-            total = total + inm[p, i]
-        mloc[0] = total.reshape(2, 8, BLOCK)
-
-        @pl.when(r == owner)
-        def _():
             for i in plane:
-                got(iny.at[p, i], yt_r.at[p, i])
-            total = iny[p, 0]
-            for i in range(1, N):
-                total = total + iny[p, i]
-            mloc[1] = total.reshape(2, 8, BLOCK)
-
-        @pl.when(r != owner)
-        def _():
-            mloc[1] = jnp.zeros((2, 8, BLOCK), F32)
-
-        go(send(mloc.at[:, other], mpair.at[p], s_r.at[p], mate, c))
-
-        for i in plane:
-            got(slot(1, i, core), t_r.at[p, 1, i, core])
-        cross[1].start()
-        for i in plane:
-            got(slot(2, i, core), t_r.at[p, 2, i, core])
-        cross[2].start()
-        got(mpair.at[p], s_r.at[p])
-        mring[p, z] = mloc[:, core] + mpair[p]
-        for q in ring:
-            go(send(mring.at[p, z], mring.at[p, z], u_r.at[p, z], 2 * q + core, c))
+                go(send(own, own, x_r.at[p, c], r, i))
+            for q in ring:
+                got(zin.at[p, q], z_r.at[p, q])
+            total = zin[p, 0]
+            for q in range(1, NZ):
+                total = total + zin[p, q]
+            mine = aec_at(spot)
+            when(r != owner, lambda: got(mine, ac_r.at[p]))
+            xc[p, at(spot, 32), :] = total + dot(mine[...], lt)
+            own = xc.at[p, at(spot, 32)]
+            for q in ring:
+                go(send(own, own, y_r.at[p, z], 2 * q + core, c))
+            go(send(own, own, w_r.at[p, z], mate, c))
+            if p == 0:
+                own = aefc.at[at(spot, 32)]
+                for q in ring:
+                    go(send(own, own, ag_r.at[z], 2 * q + core, c))
+                go(send(own, own, am_r.at[z], mate, c))
+                own = aefr.at[at(c, 32)]
+                for i in plane:
+                    go(send(own, own, af_r.at[c], r, i))
+
+        if p > 0:
+            sums()
+
         got(tall.at[p, 1, :, other], tm_r.at[p, 1])
-        got(tall.at[p, 2, :, other], tm_r.at[p, 2])
-
-        n_ref[...] = tall[p, 0].reshape(BLOCK, BLOCK) + dot(tall[p, 1].reshape(BLOCK, BLOCK), lt, (0, 0))
+        top = tall[p, 1].reshape(BLOCK, BLOCK)
+        n_ref[...] = tall[p, 0].reshape(BLOCK, BLOCK) + dot(top, lt, (0, 0))
         aug[...] = n_ref[:128, :]
         strips(aug, None, 0, 4, True)
+
+        if p == 0:
+            sums()
+
+        d0 = aug[:, :128]
+        n01 = aug[:, 128:]
+        n10d = dot(n_ref[128:, :128], d0)
+        aug2[...] = n_ref[128:, 128:] - dot(n_ref[128:, :128], n01)
+        if p == 0:
+            strips(aug2, None, 0, 2, True)
 
         for q in ring:
             got(mring.at[p, q], u_r.at[p, q])
@@ -458,24 +534,15 @@
         for q in range(1, NZ):
             total = total + mring[p, q]
         ball[p, :, c, core] = total
-        own = ball.at[p, :, c, core]
+        own_b = ball.at[p, :, c, core]
         for i in plane:
-            go(send(own, own, v_r.at[p, c], r, i))
+            go(send(own_b, own_b, v_r.at[p, c], r, i))
         for q in ring:
             part = xc.at[p, at(core * NZ + q, 32)]
             got(part, y_r.at[p, q])
             go(send(part, part, w_r.at[p, q], mate, c))
 
-        d0 = aug[:, :128]
-        n01 = aug[:, 128:]
-        n10d = dot(n_ref[128:, :128], d0)
-        aug2[...] = n_ref[128:, 128:] - dot(n_ref[128:, :128], n01)
-        strips(aug2, None, 0, 2, True)
-        for i in plane:
-            got(ball.at[p, :, i, core], v_r.at[p, i])
-        final = ball.at[p, :, :, core]
-        go(send(final, final, f_r.at[p], mate, c))
-        strips(aug2, None, 2, 4, True)
+        strips(aug2, None, 2 if p == 0 else 0, 4, True)
         e = aug2[...]
         k10 = -dot(e, n10d)
         k_ref[:128, :128] = d0 - dot(n01, k10)
@@ -483,6 +550,12 @@
         k_ref[128:, :128] = k10
         k_ref[128:, 128:] = e
 
+        if p == 0:
+            for q in ring:
+                part = aefc.at[at(core * NZ + q, 32)]
+                got(part, ag_r.at[q])
+                go(send(part, part, am_r.at[q], mate, c))
+
         zr[...] = pr[p]
         zc[...] = pc[p]
 
@@ -494,6 +567,11 @@
         def _():
             zc[off : off + BLOCK, :] = zc[off : off + BLOCK, :] + lt_ref[...]
 
+        got(tall.at[p, 2, :, other], tm_r.at[p, 2])
+        for i in plane:
+            got(ball.at[p, :, i, core], v_r.at[p, i])
+        final = ball.at[p, :, :, core]
+        go(send(final, final, f_r.at[p], mate, c))
         for i in plane:
             got(xr.at[p, at(i, 32)], x_r.at[p, i])
         for q in range(NZ):
@@ -508,29 +586,44 @@
         uc = dot(xc[p], k_ref[...]) - dot(zc[...], coupled)
         dest = out_ref if p == PANELS - 1 else cur
         dest[...] = cur[...] - dot(ur, zc[...], (1, 1)) - dot(zr[...], uc, (1, 1))
+        if p == 0:
+            ztop = top + lt
+            utop = dot(xtop, k_ref[...]) - dot(ztop, coupled)
+            rows = lax.broadcasted_iota(jnp.int32, (height, BLOCK), 0)
+            for i in plane:
+                got(aefr.at[at(i, 32)], af_r.at[i])
+            near = aefr[...] - dot(ur, ztop, (1, 1)) - dot(zr[...], utop, (1, 1))
+            pr[1] = jnp.where(r * height + rows >= lead + BLOCK, near, 0.0)
+            for q in range(NZ):
+                got(aefc.at[at(other * NZ + q, 32)], am_r.at[q])
+            near = aefc[...] - dot(uc, ztop, (1, 1)) - dot(zc[...], utop, (1, 1))
+            pc[1] = jnp.where(c * height + rows >= lead + BLOCK, near, 0.0)
 
         def left(copies):
             for copy in copies:
                 copy.wait_send()
 
         left(share[0] + share[1] + share[2] + cross + sends)
-        when(r == 0, lambda: left(g_out + down[0] + root_c))
-        when(r == owner, lambda: left(down[1] + down[2] + ae_c + y_out))
+        when(r == 0, lambda: left(g_out + down[0]))
+        when(r == owner, lambda: left(down[1] + down[2] + ae_c + y_own + [yswap]))
+        when(mate == owner, lambda: left(y_mate))
         when((r == owner) & (c == 0), lambda: left(top_out))
         when((r == owner) & (c == owner), lambda: left(ee_out))
-        when(c == 0, lambda: left(root_r))
         when(c == owner, lambda: left(ae_r))
-
-        @pl.when(c != 0)
-        def _():
-            for i, copy in ahead_r:
-                when(i != 0, copy.wait_send)
-
-        @pl.when(relay)
-        def _():
-            for q, copy in ahead_c:
-                when(q != 0, copy.wait_send)
-            left(low_c)
+        if p == 0:
+            when(r == 0, lambda: left(root_c))
+            when(c == 0, lambda: left(root_r))
+
+            @pl.when(c != 0)
+            def _():
+                for i, copy in ahead_r:
+                    when(i != 0, copy.wait_send)
+
+            @pl.when(relay)
+            def _():
+                for q, copy in ahead_c:
+                    when(q != 0, copy.wait_send)
+                left(low_c)
 
 
 def per_device(matrix):
@@ -551,8 +644,10 @@
             buf(2, 512, 256),
             buf(512, 256),
             buf(512, 256),
-            buf(2, 32, 256),
-            buf(2, 32, 256),
+            buf(32, 256),
+            buf(32, 256),
+            buf(512, 256),
+            buf(512, 256),
             buf(256, 256),
             buf(2, N, 16, 256),
             buf(2, 3, 2, 8, 256),
@@ -567,17 +662,19 @@
             buf(512, 256),
             buf(512, 256),
             buf(512, 256),
-            buf(256, 256),
+            buf(N, 2, 8, 256),
+            buf(2, N, 8, 256),
+            buf(N, 8, 256),
+            buf(N, 2, 8, 256),
+            buf(2, N, 8, 256),
             buf(2, N, 32, 256),
-            buf(2, N, 16, 256),
-            buf(2, N, 16, 256),
+            buf(2, N, 8, 256),
+            buf(2, N, 8, 256),
             buf(2, 256, 256),
             buf(NZ, 32, 256),
             buf(2, NZ, 32, 256),
             buf(2, 512, 256),
             buf(2, 512, 256),
-            buf(2, 2, 8, 256),
-            buf(2, 2, 8, 256),
             buf(2, NZ, 2, 8, 256),
             buf(2, 2, N, 2, 8, 256),
             dma((480,)),
@@ -585,13 +682,17 @@
             dma((2, 3, 2)),
             dma((2, 3, N, 2)),
             dma((2, 3)),
-            dma((2, N)),
-            dma((2, NZ)),
+            dma((N,)),
+            dma((NZ,)),
             dma((2,)),
             dma((2,)),
+            dma((N,)),
+            dma((NZ,)),
+            dma((NZ,)),
             dma((2, N)),
             dma((2, N)),
             dma((2, N)),
+            dma((2,)),
             dma((2,)),
             dma((2, NZ)),
             dma((2, N)),

time: 159 us -> 151 us (0.950)
  Pallas kernels: 156 us -> 149 us
    pallas_call x1, Pallas kernels: 156 us -> 149 us  [per_device(): pl.pallas_call(kernel, out_shape=jax.ShapeDtypeStruct(matrix.shape, F32),...]
where the time goes in v5:
time: 151 us
  Pallas kernels  149 us (99%)
  local copies, waits for them, and re-layouts  2.26 us (1%)
    pallas_call x1, Pallas kernels, per_device(): pl.pallas_call(kernel, out_shape=jax.ShapeDtypeStruct(matrix.shape, F32),...  149 us

profile of v5, /device:TPU:1, one launch (start us, length us, event | category | flops | bytes accessed | tf_op | source)
XLA Modules:
  0.0 151.3 jit_solution(18093120114111110920)
XLA Ops:
  0.0 149.1 %reduce_panels.1 = f32[512,512]{1,0:T(8,128)} custom-call(f32[512,512]{1,0:T(8,128)} %a_ref.1), custom_call_target="tpu_custom_call" | custom-call | tf_op jit(solution)/shard_map/reduce_panels/pallas_call | solution.py:635
  149.1 2.3 %copy.3 = f32[512,512]{1,0:T(8,128)} copy(f32[512,512]{1,0:T(8,128)} %reduce_panels.1) | data formatting | bytes 2097152

commit v6 on v5

v6 whole, which is shorter than its diff:
```python
import jax
import jax.numpy as jnp
from jax import lax
from jax.experimental import pallas as pl
from jax.experimental.pallas import tpu as pltpu
from jax.sharding import PartitionSpec as P

BLOCK = 256
PANELS = 2
N = 16
NZ = 8
HIGH = lax.Precision.HIGHEST
F32 = jnp.float32
MESH = pl.DeviceIdType.MESH
VMEM = pl.BlockSpec(memory_space=pltpu.VMEM)


def dot(left, right, over=(1, 0)):
    return lax.dot_general(
        left,
        right,
        (((over[0],), (over[1],)), ((), ())),
        precision=HIGH,
        preferred_element_type=F32,
    )


def dot3(left, right, over=(1, 0)):
    def split(x):
        high = x.astype(jnp.bfloat16)
        return high, (x - high.astype(F32)).astype(jnp.bfloat16)

    def part(a, b):
        return lax.dot_general(
            a, b, (((over[0],), (over[1],)), ((), ())), preferred_element_type=F32
        )

    lh, ll = split(left)
    rh, rl = split(right)
    return part(lh, rh) + (part(lh, rl) + part(ll, rh))


def recip(x):
    r = pl.reciprocal(x, approx=True)
    return r * (2.0 - x * r)


def lanes(block, index):
    return jnp.take_along_axis(block, jnp.full((8, 128), index, jnp.int32), axis=1)


def times(scale, row):
    if row.shape[1] == 128:
        return scale * row
    return jnp.concatenate([scale * row[:, :128], scale * row[:, 128:]], axis=1)


def put(rows):
    sub = lax.broadcasted_iota(jnp.int32, rows[0].shape, 0)
    out = rows[0]
    for s in range(1, 8):
        out = jnp.where(sub == s, rows[s], out)
    return out


def group(aug, out, base, inverse):
    width = aug.shape[1]
    lane = lax.broadcasted_iota(jnp.int32, (8, 128), 1)
    inside = (lane >= base) & (lane < base + 8)

    def left(block, value):
        if width == 128:
            return jnp.where(inside, value, block)
        return jnp.concatenate([jnp.where(inside, value, block[:, :128]), block[:, 128:]], axis=1)

    rows = [jnp.broadcast_to(aug[pl.ds(base + s, 1), :], (8, width)) for s in range(8)]
    e = [[None] * 8 for _ in range(8)]
    for t in range(8):
        for s in range(8 if inverse else t + 1):
            e[s][t] = lanes(rows[s][:, :128], base + t)
    if inverse:
        rows = [left(rows[s], (lane == base + s).astype(F32)) for s in range(8)]
    inv = []
    for s in range(8):
        inv.append(recip(e[s][s]))
        for t in range(s + 1, 8):
            f = (e[t][s] if inverse else e[s][t]) * inv[s]
            for u in range(s + 1 if inverse else t, 8):
                e[t][u] = e[t][u] - f * e[s][u]
            rows[t] = rows[t] - times(f, rows[s])
    if not inverse:
        out[pl.ds(base, 8), :] = put([times(lax.rsqrt(e[s][s]), rows[s]) for s in range(8)])
    solved = [None] * 8
    for s in reversed(range(8)):
        acc = rows[s]
        for t in range(s + 1, 8):
            acc = acc - times(e[s][t], solved[t])
        solved[s] = times(inv[s], acc)
    own = put(solved)
    strip = pl.multiple_of(base // 32 * 32, 32)
    blocks = [aug[pl.ds(strip + 8 * k, 8), :] for k in range(4)]
    after = [left(b, 0.0) if inverse else b for b in blocks]
    for s in range(8):
        for k in range(4):
            after[k] = after[k] - times(lanes(blocks[k][:, :128], base + s), solved[s])
    for k in range(4):
        aug[pl.ds(strip + 8 * k, 8), :] = jnp.where(strip + 8 * k == base, own, after[k])


def strips(aug, out, lo, hi, inverse):
    row = lax.broadcasted_iota(jnp.int32, (128, 128), 0) // 32
    lane = lax.broadcasted_iota(jnp.int32, (128, 128), 1) // 32

    def one(k, q):
        group(aug, out, pl.multiple_of(32 * q + 8 * k, 8), inverse)
        return q

    def strip(q, carry):
        lax.fori_loop(0, 4, one, q)
        aim = (lane == q) & ((row != q) if inverse else (row > q))
        near = aug[:, :128]
        prod = dot(jnp.where(aim, near, 0.0), aug[...])
        if inverse:
            near = jnp.where(aim, 0.0, near)
        aug[:, :128] = near - prod[:, :128]
        if aug.shape[1] > 128:
            aug[:, 128:] = aug[:, 128:] - prod[:, 128:]
        return carry

    lax.fori_loop(lo, hi, strip, 0)


def remote(src, dst, send, recv, row, col):
    return pltpu.make_async_remote_copy(
        src_ref=src,
        dst_ref=dst,
        send_sem=send,
        recv_sem=recv,
        device_id=(row, col),
        device_id_type=MESH,
    )


def greet(r, c):
    barrier = pltpu.get_barrier_semaphore()
    for k in range(1, N):
        pl.semaphore_signal(barrier, inc=1, device_id=(r, lax.rem(c + k, N)), device_id_type=MESH)
        pl.semaphore_signal(barrier, inc=1, device_id=(lax.rem(r + k, N), c), device_id_type=MESH)
    pl.semaphore_wait(barrier, 2 * (N - 1))


def at(index, size):
    return pl.ds(pl.multiple_of(index * size, size), size)


def kernel(
    a_ref, out_ref,
    cur, pr, pct, pc, aer, aec, aepr, aepc, aefr, aefc, gram, gin, tsrc, tall, lt_ref, k_ref, n_ref, aug, aug2, low,
    zr, zc, wr, wc, m, mpair, mh, ybuf, yin, inr, inm, iny, half, hsum, zin, xr, xc, mring, ball,
    ux, uy,
    ss, g_r, b_r, td_r, t_r, tm_r, pa_r, p_r, qa_r, q_r, ql_r, ar_r, ac_r, af_r, ag_r, am_r,
    r_r, m_r, yt_r, ys_r, h_r, z_r, x_r, y_r, w_r, s_r, u_r, v_r, f_r,
):
    r, c = lax.axis_index("row"), lax.axis_index("col")
    z, core = r // 2, lax.rem(r, 2)
    other = 1 - core
    mate = r + 1 - 2 * core
    height = a_ref.shape[0]
    upper = lax.broadcasted_iota(jnp.int32, (128, 128), 0) <= lax.broadcasted_iota(
        jnp.int32, (128, 128), 1
    )
    plane = [lax.rem(c + k, N) for k in range(1, N)]
    line = [lax.rem(r + k, N) for k in range(1, N)]
    ring = [lax.rem(z + k, NZ) for k in range(1, NZ)]

    def got(ref, sem):
        remote(ref, ref, ss.at[0], sem, r, c).wait_recv()

    def when(cond, run):
        pl.when(cond)(run)

    cur[...] = a_ref[...]
    zown = 0

    for p in range(PANELS):
        first, lead = p * BLOCK, (p + 1) * BLOCK
        owner, off = lead // height, lead % height
        count = iter(range(1, 60))
        sends = []

        class Group:
            def __init__(self, rows):
                self.sem = ss.at[next(count)]
                self.rows = rows
                self.copies = []

            def add(self, src, dst, sem, row, col):
                self.copies.append(remote(src, dst, self.sem, sem, row, col))
                return self.copies[-1]

            def start(self):
                for copy in self.copies:
                    copy.start()

            def left(self):
                if self.rows <= 512:
                    view = wc.at[pl.ds(0, self.rows)]
                else:
                    view = pr.at[:, pl.ds(0, self.rows // 2)]
                remote(view, view, self.sem, self.sem, r, c).wait_send()

        def group_of(rows, items):
            made = Group(rows)
            for item in items:
                made.add(*item)
            return made

        def go(made):
            made.start()
            sends.append(made)

        def slot(a, i, h):
            return tall.at[p, a, i, h]

        def aer_at(i):
            return aefr.at[at(i, 32)] if p == 0 else aepr

        def aec_at(i):
            return aefc.at[at(i, 32)] if p == 0 else aepc

        spot = core * NZ + z

        if p == 0:

            @pl.when(r == 0)
            def _():
                cols = c * height + lax.broadcasted_iota(jnp.int32, (BLOCK, height), 1)
                pct[...] = jnp.where(cols >= lead, cur[first : first + BLOCK, :], 0.0)
                gram[...] = dot(pct[...], pct[...], (1, 1))
                gin[p, c] = gram[at(c, 16), :]

            @pl.when(c == 0)
            def _():
                rows = r * height + lax.broadcasted_iota(jnp.int32, (height, BLOCK), 0)
                pr[p] = jnp.where(rows >= lead, cur[:, first : first + BLOCK], 0.0)

        else:

            @pl.when(r == 0)
            def _():
                gram[...] = dot(pc[p], pc[p], (0, 0))
                gin[p, c] = gram[at(c, 16), :]

        def row8(i, h):
            return pl.ds(pl.multiple_of(off + 16 * i + 8 * h, 8), 8)

        g_out = group_of(240, [(gram.at[at(i, 16)], gin.at[p, c], g_r.at[p], r, i) for i in plane])
        top_out = group_of(
            240,
            [(pr.at[p, row8(i, h)], tsrc.at[p, 1, h], b_r.at[p, 1], r, i) for i in plane for h in (0, 1)],
        )
        ee_out = group_of(
            240,
            [(aer.at[row8(i, h)], tsrc.at[p, 2, h], b_r.at[p, 2], r, i) for i in plane for h in (0, 1)],
        )
        down = [
            group_of(
                120,
                [
                    (tsrc.at[p, a, lax.rem(i, 2)], slot(a, c, lax.rem(i, 2)), td_r.at[p, a], i, c)
                    for i in line
                ],
            )
            for a in range(3)
        ]
        share = [
            group_of(120, [(slot(a, c, core), slot(a, c, core), t_r.at[p, a], r, i) for i in plane])
            for a in range(3)
        ]
        cross = [
            group_of(128, [(tall.at[p, a, :, core], tall.at[p, a, :, core], tm_r.at[p, a], mate, c)])
            for a in range(3)
        ]
        ae_r = group_of(480, [(aer.at[at(i, 32)], aer_at(i), ar_r.at[p], r, i) for i in plane])
        ae_c = group_of(
            480,
            [
                (aec.at[at(lax.rem(i, 2) * NZ + i // 2, 32)], aec_at(lax.rem(i, 2) * NZ + i // 2), ac_r.at[p], i, c)
                for i in line
            ],
        )
        relay = (core == 0) & (z != 0)
        if p == 0:

            def pr_part(q, sem, i):
                return (pr.at[p, at(q, 32)], pr.at[p, at(q, 32)], sem.at[0], r, i)

            def pc_part(q, sem, row):
                return (pc.at[p, at(q, 64)], pc.at[p, at(q, 64)], sem.at[0], row, c)

            root_r = group_of(
                960,
                [pr_part(i, pa_r, i) for i in range(1, N)] + [pr_part(0, p_r, i) for i in range(1, N)],
            )
            root_c = group_of(
                896,
                [pc_part(q, qa_r, 2 * q) for q in range(1, NZ)]
                + [pc_part(0, q_r, 2 * q) for q in range(1, NZ)],
            )
            ahead_r = group_of(448, [pr_part(c, p_r, i) for i in plane])
            ahead_c = group_of(384, [pc_part(z, q_r, 2 * q) for q in ring])
            low_c = group_of(512, [(pc.at[p], pc.at[p], ql_r.at[0], r + 1, c)])

        @pl.when(c == owner)
        def _():
            aer[...] = cur[:, off : off + BLOCK]
            mine = aer[at(c, 32), :]
            if p == 0:
                aefr[at(c, 32), :] = mine
            else:
                aepr[...] = mine

        @pl.when(r == owner)
        def _():
            aec[...] = cur[off : off + BLOCK, :].T
            mine = aec[at(spot, 32), :]
            if p == 0:
                aefc[at(spot, 32), :] = mine
            else:
                aepc[...] = mine

        if p == 0:
            greet(r, c)

        when(r == 0, g_out.start)

        @pl.when((r == owner) & (c == 0))
        def _():
            for h in (0, 1):
                tsrc[p, 1, h] = pr[p, row8(c, h), :]

        @pl.when((r == owner) & (c == owner))
        def _():
            for h in (0, 1):
                tsrc[p, 2, h] = aer[row8(c, h), :]

        if p == 0:
            when((c == 0) & (r > 1), root_r.start)

        swap = group_of(256, [(wc.at[at(other, 256)], half.at[p], h_r.at[p], mate, c)])
        mswap = group_of(128, [(m.at[:, other], mpair.at[p], s_r.at[p], mate, c)])
        yswap = group_of(128, [(ybuf.at[:, other], yin.at[p], ys_r.at[p], mate, c)])
        y_own = group_of(120, [(ybuf.at[i, core], iny.at[p, c], yt_r.at[p], r, i) for i in plane])
        y_mate = group_of(120, [(yin.at[p, i], iny.at[p, c], yt_r.at[p], r, i) for i in plane])

        def products():
            wc[...] = dot3(cur[...], pr[p], (0, 0))
            go(swap)
            wr[...] = dot3(cur[...], pc[p])

            @pl.when(r == owner)
            def _():
                ybuf[...] = wr[off : off + BLOCK, :].reshape(N, 2, 8, BLOCK)
                yswap.start()

            m[...] = dot(pr[p], wr[...], (0, 0)).reshape(N, 2, 8, BLOCK)
            go(mswap)

        def scatter():
            got(mpair.at[p], s_r.at[p])
            mh[...] = m[:, core] + mpair[p]
            go(group_of(120, [(mh.at[i], inm.at[p, c], m_r.at[p], r, i) for i in plane]))
            inm[p, c] = mh[c]

            @pl.when(r == owner)
            def _():
                y_own.start()
                iny[p, c] = ybuf[c, core]

            @pl.when(mate == owner)
            def _():
                got(yin.at[p], ys_r.at[p])
                y_mate.start()
                iny[p, c] = yin[p, c]

            go(group_of(480, [(wr.at[at(i, 32)], inr.at[p, c], r_r.at[p], r, i) for i in plane]))
            inr[p, c] = wr[at(c, 32), :]
            got(half.at[p], h_r.at[p])
            hsum[...] = (wc[at(core, 256), :] + half[p]).reshape(NZ, 32, BLOCK)
            zin[p, z] = hsum[z]
            go(group_of(224, [(hsum.at[q], zin.at[p, z], z_r.at[p], 2 * q + core, c) for q in ring]))

        if p > 0:
            products()

        @pl.when(r == 0)
        def _():
            got(gin.at[p, pl.ds(0, N - 1)], g_r.at[p])
            total = gin[p, 0]
            for i in range(1, N):
                total = total + gin[p, i]
            tsrc[p, 0] = total.reshape(2, 8, BLOCK)
            tall[p, 0, c, core] = tsrc[p, 0, core]
            down[0].start()

        when((r == owner) & (c == 0), top_out.start)
        when((r == owner) & (c == owner), ee_out.start)
        when(r != 0, lambda: got(slot(0, c, core), td_r.at[p, 0]))
        share[0].start()

        if p == 0:
            when((c == 0) & (r <= 1), root_r.start)

            @pl.when(r == 0)
            def _():
                pc[p] = pct[...].T
                root_c.start()
                low_c.start()

            @pl.when(relay)
            def _():
                got(pc.at[p, at(z, 64)], qa_r.at[0])
                for q, copy in zip(ring, ahead_c.copies):
                    when(q != 0, copy.start)

        @pl.when(r == owner)
        def _():
            for a, holder in ((1, 0), (2, owner)):
                when(c != holder, lambda a=a: got(tsrc.at[p, a], b_r.at[p, a]))
                tall[p, a, c, core] = tsrc[p, a, core]
                down[a].start()

        def slots(a):
            return tall.at[p, a, pl.ds(0, N - 1), core]

        got(slots(0), t_r.at[p, 0])
        cross[0].start()

        if p == 0:

            @pl.when(c != 0)
            def _():
                got(pr.at[p, at(c, 32)], pa_r.at[0])
                for i, copy in zip(plane, ahead_r.copies):
                    when(i != 0, copy.start)

        else:
            scatter()

        when(c == owner, ae_r.start)
        when(r == owner, ae_c.start)
        got(tall.at[p, 0, :, other], tm_r.at[p, 0])

        g = tall[p, 0].reshape(BLOCK, BLOCK)
        aug[...] = g[:128, :]
        strips(aug, lt_ref, 0, 4, False)
        lt_ref[:128, :128] = jnp.where(upper, lt_ref[:128, :128], 0.0)
        lt01 = lt_ref[:128, 128:]
        aug2[...] = g[128:, 128:] - dot(lt01, lt01, (0, 0))
        lt_ref[128:, :128] = jnp.zeros((128, 128), F32)

        for a in (1, 2):
            when(r != owner, lambda a=a: got(slot(a, c, core), td_r.at[p, a]))
            share[a].start()

        if p == 0:

            @pl.when(relay)
            def _():
                got(pc.at[p, pl.ds(0, 448)], q_r.at[0])
                low_c.start()

            @pl.when(c != 0)
            def _():
                got(pr.at[p, pl.ds(0, 480)], p_r.at[0])

            when(core == 1, lambda: got(pc.at[p], ql_r.at[0]))
            products()
            scatter()

        strips(aug2, low, 0, 4, False)
        lt_ref[128:, 128:] = jnp.where(upper, low[...], 0.0)
        lt = lt_ref[...]

        for a in (1, 2):
            got(slots(a), t_r.at[p, a])
            cross[a].start()

        def sum_m():
            got(inm.at[p, pl.ds(0, N - 1)], m_r.at[p])
            total = inm[p, 0]
            for i in range(1, N):
                total = total + inm[p, i]
            mring[p, z, 0] = total

            @pl.when(z == zown)
            def _():
                got(iny.at[p, pl.ds(0, N - 1)], yt_r.at[p])
                total = iny[p, 0]
                for i in range(1, N):
                    total = total + iny[p, i]
                mring[p, z, 1] = total

            @pl.when(z != zown)
            def _():
                mring[p, z, 1] = jnp.zeros((8, BLOCK), F32)

            go(group_of(112, [(mring.at[p, z], mring.at[p, z], u_r.at[p], 2 * q + core, c) for q in ring]))

        def sum_x():
            got(inr.at[p, pl.ds(0, N - 1)], r_r.at[p])
            total = inr[p, 0]
            for i in range(1, N):
                total = total + inr[p, i]
            mine = aer_at(c)
            when(c != owner, lambda: got(mine, ar_r.at[p]))
            xr[p, at(c, 32), :] = total + dot(mine[...], lt)
            own = xr.at[p, at(c, 32)]
            go(group_of(480, [(own, own, x_r.at[p], r, i) for i in plane]))
            got(zin.at[p, pl.ds(0, NZ - 1)], z_r.at[p])
            total = zin[p, 0]
            for q in range(1, NZ):
                total = total + zin[p, q]
            mine_c = aec_at(spot)
            when(r != owner, lambda: got(mine_c, ac_r.at[p]))
            xc[p, at(spot, 32), :] = total + dot(mine_c[...], lt)
            own_c = xc.at[p, at(spot, 32)]
            go(group_of(224, [(own_c, own_c, y_r.at[p], 2 * q + core, c) for q in ring]))
            if p == 0:
                own_c = aefc.at[at(spot, 32)]
                go(group_of(224, [(own_c, own_c, ag_r.at[0], 2 * q + core, c) for q in ring]))
                own = aefr.at[at(c, 32)]
                go(group_of(480, [(own, own, af_r.at[0], r, i) for i in plane]))

        sum_m()
        if p > 0:
            sum_x()

        got(tall.at[p, 1, :, other], tm_r.at[p, 1])
        top = tall[p, 1].reshape(BLOCK, BLOCK)
        n_ref[...] = tall[p, 0].reshape(BLOCK, BLOCK) + dot(top, lt, (0, 0))
        aug[...] = n_ref[:128, :]
        strips(aug, None, 0, 4, True)

        if p == 0:
            sum_x()

        d0 = aug[:, :128]
        n01 = aug[:, 128:]
        n10d = dot(n_ref[128:, :128], d0)
        aug2[...] = n_ref[128:, 128:] - dot(n_ref[128:, :128], n01)
        strips(aug2, None, 0, 2, True)

        got(mring.at[p, pl.ds(0, NZ - 1)], u_r.at[p])
        total = mring[p, 0]
        for q in range(1, NZ):
            total = total + mring[p, q]
        ball[p, :, c, core] = total
        own_b = ball.at[p, :, c, core]
        go(group_of(240, [(own_b, own_b, v_r.at[p], r, i) for i in plane]))

        strips(aug2, None, 2, 4, True)
        part = xc.at[p, at(core, 256)]
        got(xc.at[p, pl.ds(0, 224)], y_r.at[p])
        go(group_of(256, [(part, part, w_r.at[p], mate, c)]))
        e = aug2[...]
        k10 = -dot(e, n10d)
        k_ref[:128, :128] = d0 - dot(n01, k10)
        k_ref[:128, 128:] = -dot(n01, e)
        k_ref[128:, :128] = k10
        k_ref[128:, 128:] = e

        zr[...] = pr[p]
        zc[...] = pc[p]

        @pl.when(r == owner)
        def _():
            zr[off : off + BLOCK, :] = zr[off : off + BLOCK, :] + lt_ref[...]

        @pl.when(c == owner)
        def _():
            zc[off : off + BLOCK, :] = zc[off : off + BLOCK, :] + lt_ref[...]

        got(tall.at[p, 2, :, other], tm_r.at[p, 2])
        got(ball.at[p, :, pl.ds(0, N - 1), core], v_r.at[p])
        final = ball.at[p, :, :, core]
        go(group_of(256, [(final, final, f_r.at[p], mate, c)]))
        got(xr.at[p, pl.ds(0, 480)], x_r.at[p])
        ux[...] = dot3(xr[p], k_ref[...])
        got(xc.at[p, pl.ds(0, 256)], w_r.at[p])
        uy[...] = dot3(xc[p], k_ref[...])
        if p == 0:
            part = aefc.at[at(core, 256)]
            got(aefc.at[pl.ds(0, 224)], ag_r.at[0])
            go(group_of(256, [(part, part, am_r.at[0], mate, c)]))
        got(ball.at[p, :, :, other], f_r.at[p])

        ytop = ball[p, 1].reshape(BLOCK, BLOCK)
        xtop = ytop + dot(tall[p, 2].reshape(BLOCK, BLOCK), lt)
        inner = ball[p, 0].reshape(BLOCK, BLOCK) + dot(ytop, lt, (0, 0)) + dot(lt, xtop, (0, 0))
        coupled = 0.5 * dot(k_ref[...], dot(inner, k_ref[...]), (0, 0))
        ur = ux[...] - dot3(zr[...], coupled)
        uc = uy[...] - dot3(zc[...], coupled)
        dest = out_ref if p == PANELS - 1 else cur
        dest[...] = cur[...] - dot3(ur, zc[...], (1, 1)) - dot3(zr[...], uc, (1, 1))
        if p == 0:
            ztop = top + lt
            utop = dot(xtop, k_ref[...]) - dot(ztop, coupled)
            rows = lax.broadcasted_iota(jnp.int32, (height, BLOCK), 0)
            got(aefr.at[pl.ds(0, 480)], af_r.at[0])
            near = aefr[...] - dot3(ur, ztop, (1, 1)) - dot3(zr[...], utop, (1, 1))
            pr[1] = jnp.where(r * height + rows >= lead + BLOCK, near, 0.0)
            got(aefc.at[pl.ds(0, 256)], am_r.at[0])
            near = aefc[...] - dot3(uc, ztop, (1, 1)) - dot3(zc[...], utop, (1, 1))
            pc[1] = jnp.where(c * height + rows >= lead + BLOCK, near, 0.0)

        for made in sends + share + cross:
            made.left()
        when(r == 0, g_out.left)
        when(r == 0, down[0].left)
        for made in (down[1], down[2], ae_c, y_own, yswap):
            when(r == owner, made.left)
        when(mate == owner, y_mate.left)
        when((r == owner) & (c == 0), top_out.left)
        when((r == owner) & (c == owner), ee_out.left)
        when(c == owner, ae_r.left)
        if p == 0:
            when(r == 0, root_c.left)
            when(c == 0, root_r.left)
            when(c != 0, ahead_r.left)
            when(relay, ahead_c.left)
            when(core == 0, low_c.left)


def per_device(matrix):
    dma = pltpu.SemaphoreType.DMA

    def buf(*shape):
        return pltpu.VMEM(shape, F32)

    return pl.pallas_call(
        kernel,
        out_shape=jax.ShapeDtypeStruct(matrix.shape, F32),
        in_specs=[VMEM],
        out_specs=VMEM,
        scratch_shapes=[
            buf(512, 512),
            buf(2, 512, 256),
            buf(256, 512),
            buf(2, 512, 256),
            buf(512, 256),
            buf(512, 256),
            buf(32, 256),
            buf(32, 256),
            buf(512, 256),
            buf(512, 256),
            buf(256, 256),
            buf(2, N, 16, 256),
            buf(2, 3, 2, 8, 256),
            buf(2, 3, N, 2, 8, 256),
            buf(256, 256),
            buf(256, 256),
            buf(256, 256),
            buf(128, 256),
            buf(128, 128),
            buf(128, 128),
            buf(512, 256),
            buf(512, 256),
            buf(512, 256),
            buf(512, 256),
            buf(N, 2, 8, 256),
            buf(2, N, 8, 256),
            buf(N, 8, 256),
            buf(N, 2, 8, 256),
            buf(2, N, 8, 256),
            buf(2, N, 32, 256),
            buf(2, N, 8, 256),
            buf(2, N, 8, 256),
            buf(2, 256, 256),
            buf(NZ, 32, 256),
            buf(2, NZ, 32, 256),
            buf(2, 512, 256),
            buf(2, 512, 256),
            buf(2, NZ, 2, 8, 256),
            buf(2, 2, N, 2, 8, 256),
            buf(512, 256),
            buf(512, 256),
            dma((60,)),
            dma((2,)),
            dma((2, 3)),
            dma((2, 3)),
            dma((2, 3)),
            dma((2, 3)),
            dma((1,)),
            dma((1,)),
            dma((1,)),
            dma((1,)),
            dma((1,)),
            dma((2,)),
            dma((2,)),
            dma((1,)),
            dma((1,)),
            dma((1,)),
            dma((2,)),
            dma((2,)),
            dma((2,)),
            dma((2,)),
            dma((2,)),
            dma((2,)),
            dma((2,)),
            dma((2,)),
            dma((2,)),
            dma((2,)),
            dma((2,)),
            dma((2,)),
            dma((2,)),
        ],
        compiler_params=pltpu.CompilerParams(collective_id=0, has_side_effects=True),
        name="reduce_panels",
    )(matrix)


def solution(mesh):
    return jax.shard_map(
        per_device, mesh=mesh, in_specs=(P("row", "col"),), out_specs=P("row", "col"), check_vma=False
    )
```

time: 151 us -> 138 us (0.914)
  Pallas kernels: 149 us -> 136 us
    pallas_call x1, Pallas kernels: 149 us -> 136 us  [per_device(): pl.pallas_call(kernel, out_shape=jax.ShapeDtypeStruct(matrix.shape, F32),...]
where the time goes in v6:
time: 138 us
  Pallas kernels  136 us (99%)
  local copies, waits for them, and re-layouts  2.26 us (2%)
    pallas_call x1, Pallas kernels, per_device(): pl.pallas_call(kernel, out_shape=jax.ShapeDtypeStruct(matrix.shape, F32),...  136 us

profile of v6, /device:TPU:1, one launch (start us, length us, event | category | flops | bytes accessed | tf_op | source)
XLA Modules:
  0.0 138.0 jit_solution(6282188640470457032)
XLA Ops:
  0.0 135.7 %reduce_panels.1 = f32[512,512]{1,0:T(8,128)} custom-call(f32[512,512]{1,0:T(8,128)} %a_ref.1), custom_call_target="tpu_custom_call" | custom-call | tf_op jit(solution)/shard_map/reduce_panels/pallas_call | solution.py:641
  135.7 2.3 %copy.3 = f32[512,512]{1,0:T(8,128)} copy(f32[512,512]{1,0:T(8,128)} %reduce_panels.1) | data formatting | bytes 2097152

commit v7 on v6

--- a/solution.py
+++ b/solution.py
@@ -344,8 +344,10 @@
             for h in (0, 1):
                 tsrc[p, 2, h] = aer[row8(c, h), :]
 
-        if p == 0:
-            when((c == 0) & (r > 1), root_r.start)
+        when((r == owner) & (c == 0), top_out.start)
+        when((r == owner) & (c == owner), ee_out.start)
+        if p == 0:
+            when(c == 0, root_r.start)
 
         swap = group_of(256, [(wc.at[at(other, 256)], half.at[p], h_r.at[p], mate, c)])
         mswap = group_of(128, [(m.at[:, other], mpair.at[p], s_r.at[p], mate, c)])
@@ -356,6 +358,8 @@
         def products():
             wc[...] = dot3(cur[...], pr[p], (0, 0))
             go(swap)
+            if p == 0:
+                when(core == 1, lambda: got(pc.at[p], ql_r.at[0]))
             wr[...] = dot3(cur[...], pc[p])
 
             @pl.when(r == owner)
@@ -403,26 +407,6 @@
             tall[p, 0, c, core] = tsrc[p, 0, core]
             down[0].start()
 
-        when((r == owner) & (c == 0), top_out.start)
-        when((r == owner) & (c == owner), ee_out.start)
-        when(r != 0, lambda: got(slot(0, c, core), td_r.at[p, 0]))
-        share[0].start()
-
-        if p == 0:
-            when((c == 0) & (r <= 1), root_r.start)
-
-            @pl.when(r == 0)
-            def _():
-                pc[p] = pct[...].T
-                root_c.start()
-                low_c.start()
-
-            @pl.when(relay)
-            def _():
-                got(pc.at[p, at(z, 64)], qa_r.at[0])
-                for q, copy in zip(ring, ahead_c.copies):
-                    when(q != 0, copy.start)
-
         @pl.when(r == owner)
         def _():
             for a, holder in ((1, 0), (2, owner)):
@@ -430,6 +414,30 @@
                 tall[p, a, c, core] = tsrc[p, a, core]
                 down[a].start()
 
+        when(r != 0, lambda: got(slot(0, c, core), td_r.at[p, 0]))
+        share[0].start()
+
+        if p == 0:
+            @pl.when(r == 0)
+            def _():
+                pc[p] = pct[...].T
+                root_c.start()
+                low_c.start()
+
+            @pl.when(relay)
+            def _():
+                got(pc.at[p, at(z, 64)], qa_r.at[0])
+                for q, copy in zip(ring, ahead_c.copies):
+                    when(q != 0, copy.start)
+
+        def share_rest():
+            for a in (1, 2):
+                when(r != owner, lambda a=a: got(slot(a, c, core), td_r.at[p, a]))
+                share[a].start()
+
+        if p > 0:
+            share_rest()
+
         def slots(a):
             return tall.at[p, a, pl.ds(0, N - 1), core]
 
@@ -444,11 +452,13 @@
                 for i, copy in zip(plane, ahead_r.copies):
                     when(i != 0, copy.start)
 
+            share_rest()
+
         else:
             scatter()
-
-        when(c == owner, ae_r.start)
-        when(r == owner, ae_c.start)
+            when(c == owner, ae_r.start)
+            when(r == owner, ae_c.start)
+
         got(tall.at[p, 0, :, other], tm_r.at[p, 0])
 
         g = tall[p, 0].reshape(BLOCK, BLOCK)
@@ -459,9 +469,13 @@
         aug2[...] = g[128:, 128:] - dot(lt01, lt01, (0, 0))
         lt_ref[128:, :128] = jnp.zeros((128, 128), F32)
 
-        for a in (1, 2):
-            when(r != owner, lambda a=a: got(slot(a, c, core), td_r.at[p, a]))
-            share[a].start()
+        def cross_rest():
+            for a in (1, 2):
+                got(slots(a), t_r.at[p, a])
+                cross[a].start()
+
+        if p > 0:
+            cross_rest()
 
         if p == 0:
 
@@ -474,17 +488,14 @@
             def _():
                 got(pr.at[p, pl.ds(0, 480)], p_r.at[0])
 
-            when(core == 1, lambda: got(pc.at[p], ql_r.at[0]))
             products()
             scatter()
+            when(c == owner, ae_r.start)
+            when(r == owner, ae_c.start)
 
         strips(aug2, low, 0, 4, False)
         lt_ref[128:, 128:] = jnp.where(upper, low[...], 0.0)
         lt = lt_ref[...]
-
-        for a in (1, 2):
-            got(slots(a), t_r.at[p, a])
-            cross[a].start()
 
         def sum_m():
             got(inm.at[p, pl.ds(0, N - 1)], m_r.at[p])
@@ -532,16 +543,21 @@
                 own = aefr.at[at(c, 32)]
                 go(group_of(480, [(own, own, af_r.at[0], r, i) for i in plane]))
 
-        sum_m()
-        if p > 0:
-            sum_x()
+        if p == 0:
+            cross_rest()
+        else:
+            sum_m()
 
         got(tall.at[p, 1, :, other], tm_r.at[p, 1])
         top = tall[p, 1].reshape(BLOCK, BLOCK)
         n_ref[...] = tall[p, 0].reshape(BLOCK, BLOCK) + dot(top, lt, (0, 0))
         aug[...] = n_ref[:128, :]
-        strips(aug, None, 0, 4, True)
-
+        strips(aug, None, 0, 2, True)
+        if p == 0:
+            sum_m()
+        else:
+            sum_x()
+        strips(aug, None, 2, 4, True)
         if p == 0:
             sum_x()
 

time: 138 us -> 128 us (0.928)
  Pallas kernels: 136 us -> 126 us
    pallas_call x1, Pallas kernels: 136 us -> 126 us  [per_device(): pl.pallas_call(kernel, out_shape=jax.ShapeDtypeStruct(matrix.shape, F32),...]
where the time goes in v7:
time: 128 us
  Pallas kernels  126 us (98%)
  local copies, waits for them, and re-layouts  2.26 us (2%)
    pallas_call x1, Pallas kernels, per_device(): pl.pallas_call(kernel, out_shape=jax.ShapeDtypeStruct(matrix.shape, F32),...  126 us

profile of v7, /device:TPU:1, one launch (start us, length us, event | category | flops | bytes accessed | tf_op | source)
XLA Modules:
  0.0 128.0 jit_solution(3398969337968728388)
XLA Ops:
  0.0 125.8 %reduce_panels.1 = f32[512,512]{1,0:T(8,128)} custom-call(f32[512,512]{1,0:T(8,128)} %a_ref.1), custom_call_target="tpu_custom_call" | custom-call | tf_op jit(solution)/shard_map/reduce_panels/pallas_call | solution.py:657
  125.8 2.3 %copy.3 = f32[512,512]{1,0:T(8,128)} copy(f32[512,512]{1,0:T(8,128)} %reduce_panels.1) | data formatting | bytes 2097152

commit v8 on v7

--- a/solution.py
+++ b/solution.py
@@ -298,10 +298,8 @@
             def pc_part(q, sem, row):
                 return (pc.at[p, at(q, 64)], pc.at[p, at(q, 64)], sem.at[0], row, c)
 
-            root_r = group_of(
-                960,
-                [pr_part(i, pa_r, i) for i in range(1, N)] + [pr_part(0, p_r, i) for i in range(1, N)],
-            )
+            root_r = group_of(480, [pr_part(i, pa_r, i) for i in range(1, N)])
+            root_own = group_of(480, [pr_part(0, p_r, i) for i in range(1, N)])
             root_c = group_of(
                 896,
                 [pc_part(q, qa_r, 2 * q) for q in range(1, NZ)]
@@ -407,15 +405,20 @@
             tall[p, 0, c, core] = tsrc[p, 0, core]
             down[0].start()
 
-        @pl.when(r == owner)
-        def _():
-            for a, holder in ((1, 0), (2, owner)):
-                when(c != holder, lambda a=a: got(tsrc.at[p, a], b_r.at[p, a]))
-                tall[p, a, c, core] = tsrc[p, a, core]
-                down[a].start()
-
+        def own_rest():
+            @pl.when(r == owner)
+            def _():
+                for a, holder in ((1, 0), (2, owner)):
+                    when(c != holder, lambda a=a: got(tsrc.at[p, a], b_r.at[p, a]))
+                    tall[p, a, c, core] = tsrc[p, a, core]
+                    down[a].start()
+
+        if p > 0:
+            own_rest()
         when(r != 0, lambda: got(slot(0, c, core), td_r.at[p, 0]))
         share[0].start()
+        if p == 0:
+            own_rest()
 
         if p == 0:
             @pl.when(r == 0)
@@ -445,6 +448,8 @@
         cross[0].start()
 
         if p == 0:
+
+            when(c == 0, root_own.start)
 
             @pl.when(c != 0)
             def _():
@@ -537,11 +542,6 @@
             xc[p, at(spot, 32), :] = total + dot(mine_c[...], lt)
             own_c = xc.at[p, at(spot, 32)]
             go(group_of(224, [(own_c, own_c, y_r.at[p], 2 * q + core, c) for q in ring]))
-            if p == 0:
-                own_c = aefc.at[at(spot, 32)]
-                go(group_of(224, [(own_c, own_c, ag_r.at[0], 2 * q + core, c) for q in ring]))
-                own = aefr.at[at(c, 32)]
-                go(group_of(480, [(own, own, af_r.at[0], r, i) for i in plane]))
 
         if p == 0:
             cross_rest()
@@ -565,16 +565,22 @@
         n01 = aug[:, 128:]
         n10d = dot(n_ref[128:, :128], d0)
         aug2[...] = n_ref[128:, 128:] - dot(n_ref[128:, :128], n01)
+        def hand_out():
+            got(mring.at[p, pl.ds(0, NZ - 1)], u_r.at[p])
+            total = mring[p, 0]
+            for q in range(1, NZ):
+                total = total + mring[p, q]
+            ball[p, :, c, core] = total
+            own_b = ball.at[p, :, c, core]
+            go(group_of(240, [(own_b, own_b, v_r.at[p], r, i) for i in plane]))
+
         strips(aug2, None, 0, 2, True)
-
-        got(mring.at[p, pl.ds(0, NZ - 1)], u_r.at[p])
-        total = mring[p, 0]
-        for q in range(1, NZ):
-            total = total + mring[p, q]
-        ball[p, :, c, core] = total
-        own_b = ball.at[p, :, c, core]
-        go(group_of(240, [(own_b, own_b, v_r.at[p], r, i) for i in plane]))
-
+        hand_out()
+        if p == 0:
+            own_c = aefc.at[at(spot, 32)]
+            go(group_of(224, [(own_c, own_c, ag_r.at[0], 2 * q + core, c) for q in ring]))
+            own = aefr.at[at(c, 32)]
+            go(group_of(480, [(own, own, af_r.at[0], r, i) for i in plane]))
         strips(aug2, None, 2, 4, True)
         part = xc.at[p, at(core, 256)]
         got(xc.at[p, pl.ds(0, 224)], y_r.at[p])
@@ -605,15 +611,15 @@
         ux[...] = dot3(xr[p], k_ref[...])
         got(xc.at[p, pl.ds(0, 256)], w_r.at[p])
         uy[...] = dot3(xc[p], k_ref[...])
+        got(ball.at[p, :, :, other], f_r.at[p])
+
+        ytop = ball[p, 1].reshape(BLOCK, BLOCK)
+        xtop = ytop + dot(tall[p, 2].reshape(BLOCK, BLOCK), lt)
+        inner = ball[p, 0].reshape(BLOCK, BLOCK) + dot(ytop, lt, (0, 0)) + dot(lt, xtop, (0, 0))
         if p == 0:
             part = aefc.at[at(core, 256)]
             got(aefc.at[pl.ds(0, 224)], ag_r.at[0])
             go(group_of(256, [(part, part, am_r.at[0], mate, c)]))
-        got(ball.at[p, :, :, other], f_r.at[p])
-
-        ytop = ball[p, 1].reshape(BLOCK, BLOCK)
-        xtop = ytop + dot(tall[p, 2].reshape(BLOCK, BLOCK), lt)
-        inner = ball[p, 0].reshape(BLOCK, BLOCK) + dot(ytop, lt, (0, 0)) + dot(lt, xtop, (0, 0))
         coupled = 0.5 * dot(k_ref[...], dot(inner, k_ref[...]), (0, 0))
         ur = ux[...] - dot3(zr[...], coupled)
         uc = uy[...] - dot3(zc[...], coupled)
@@ -643,6 +649,7 @@
         if p == 0:
             when(r == 0, root_c.left)
             when(c == 0, root_r.left)
+            when(c == 0, root_own.left)
             when(c != 0, ahead_r.left)
             when(relay, ahead_c.left)
             when(core == 0, low_c.left)

time: 128 us -> 122 us (0.953)
  Pallas kernels: 126 us -> 120 us
    pallas_call x1, Pallas kernels: 126 us -> 120 us  [per_device(): pl.pallas_call(kernel, out_shape=jax.ShapeDtypeStruct(matrix.shape, F32),...]
where the time goes in v8:
time: 122 us
  Pallas kernels  120 us (98%)
  local copies, waits for them, and re-layouts  2.26 us (2%)
    pallas_call x1, Pallas kernels, per_device(): pl.pallas_call(kernel, out_shape=jax.ShapeDtypeStruct(matrix.shape, F32),...  120 us

profile of v8, /device:TPU:1, one launch (start us, length us, event | category | flops | bytes accessed | tf_op | source)
XLA Modules:
  0.0 122.3 jit_solution(17508563113425729320)
XLA Ops:
  0.0 120.0 %reduce_panels.1 = f32[512,512]{1,0:T(8,128)} custom-call(f32[512,512]{1,0:T(8,128)} %a_ref.1), custom_call_target="tpu_custom_call" | custom-call | tf_op jit(solution)/shard_map/reduce_panels/pallas_call | solution.py:664
  120.0 2.3 %copy.3 = f32[512,512]{1,0:T(8,128)} copy(f32[512,512]{1,0:T(8,128)} %reduce_panels.1) | data formatting | bytes 2097152

commit v9 on v8

--- a/solution.py
+++ b/solution.py
@@ -365,7 +365,7 @@
                 ybuf[...] = wr[off : off + BLOCK, :].reshape(N, 2, 8, BLOCK)
                 yswap.start()
 
-            m[...] = dot(pr[p], wr[...], (0, 0)).reshape(N, 2, 8, BLOCK)
+            m[...] = dot3(pr[p], wr[...], (0, 0)).reshape(N, 2, 8, BLOCK)
             go(mswap)
 
         def scatter():
@@ -574,9 +574,11 @@
             own_b = ball.at[p, :, c, core]
             go(group_of(240, [(own_b, own_b, v_r.at[p], r, i) for i in plane]))
 
+        if p > 0:
+            hand_out()
         strips(aug2, None, 0, 2, True)
-        hand_out()
-        if p == 0:
+        if p == 0:
+            hand_out()
             own_c = aefc.at[at(spot, 32)]
             go(group_of(224, [(own_c, own_c, ag_r.at[0], 2 * q + core, c) for q in ring]))
             own = aefr.at[at(c, 32)]
@@ -614,20 +616,20 @@
         got(ball.at[p, :, :, other], f_r.at[p])
 
         ytop = ball[p, 1].reshape(BLOCK, BLOCK)
-        xtop = ytop + dot(tall[p, 2].reshape(BLOCK, BLOCK), lt)
-        inner = ball[p, 0].reshape(BLOCK, BLOCK) + dot(ytop, lt, (0, 0)) + dot(lt, xtop, (0, 0))
+        xtop = ytop + dot3(tall[p, 2].reshape(BLOCK, BLOCK), lt)
+        inner = ball[p, 0].reshape(BLOCK, BLOCK) + dot3(ytop, lt, (0, 0)) + dot3(lt, xtop, (0, 0))
         if p == 0:
             part = aefc.at[at(core, 256)]
             got(aefc.at[pl.ds(0, 224)], ag_r.at[0])
             go(group_of(256, [(part, part, am_r.at[0], mate, c)]))
-        coupled = 0.5 * dot(k_ref[...], dot(inner, k_ref[...]), (0, 0))
+        coupled = 0.5 * dot3(k_ref[...], dot3(inner, k_ref[...]), (0, 0))
         ur = ux[...] - dot3(zr[...], coupled)
         uc = uy[...] - dot3(zc[...], coupled)
         dest = out_ref if p == PANELS - 1 else cur
         dest[...] = cur[...] - dot3(ur, zc[...], (1, 1)) - dot3(zr[...], uc, (1, 1))
         if p == 0:
             ztop = top + lt
-            utop = dot(xtop, k_ref[...]) - dot(ztop, coupled)
+            utop = dot3(xtop, k_ref[...]) - dot3(ztop, coupled)
             rows = lax.broadcasted_iota(jnp.int32, (height, BLOCK), 0)
             got(aefr.at[pl.ds(0, 480)], af_r.at[0])
             near = aefr[...] - dot3(ur, ztop, (1, 1)) - dot3(zr[...], utop, (1, 1))

time: 122 us -> 121 us (level)
  Pallas kernels: 120 us -> 118 us
    pallas_call x1, Pallas kernels: 120 us -> 118 us  [per_device(): pl.pallas_call(kernel, out_shape=jax.ShapeDtypeStruct(matrix.shape, F32),...]
where the time goes in v9:
time: 121 us
  Pallas kernels  118 us (98%)
  local copies, waits for them, and re-layouts  2.26 us (2%)
    pallas_call x1, Pallas kernels, per_device(): pl.pallas_call(kernel, out_shape=jax.ShapeDtypeStruct(matrix.shape, F32),...  118 us

profile of v9, /device:TPU:1, one launch (start us, length us, event | category | flops | bytes accessed | tf_op | source)
XLA Modules:
  0.0 120.6 jit_solution(8923032931562194031)
XLA Ops:
  0.0 118.3 %reduce_panels.1 = f32[512,512]{1,0:T(8,128)} custom-call(f32[512,512]{1,0:T(8,128)} %a_ref.1), custom_call_target="tpu_custom_call" | custom-call | tf_op jit(solution)/shard_map/reduce_panels/pallas_call | solution.py:666
  118.3 2.3 %copy.3 = f32[512,512]{1,0:T(8,128)} copy(f32[512,512]{1,0:T(8,128)} %reduce_panels.1) | data formatting | bytes 2097152

commit v10 on v9

--- a/solution.py
+++ b/solution.py
@@ -169,7 +169,9 @@
     upper = lax.broadcasted_iota(jnp.int32, (128, 128), 0) <= lax.broadcasted_iota(
         jnp.int32, (128, 128), 1
     )
-    plane = [lax.rem(c + k, N) for k in range(1, N)]
+    steps = [(2, 2), (2, 1), (1, 2), (2, 3), (3, 2), (1, 1), (3, 3), (1, 3), (3, 1), (2, 0), (0, 2)]
+    steps += [(1, 0), (0, 1), (3, 0), (0, 3)]
+    plane = [lax.rem(c // 4 + dy, 4) * 4 + lax.rem(lax.rem(c, 4) + dx, 4) for dy, dx in steps]
     line = [lax.rem(r + k, N) for k in range(1, N)]
     ring = [lax.rem(z + k, NZ) for k in range(1, NZ)]
 

time: 121 us -> 120 us (level)
  no operation moved by 1% of the time
where the time goes in v10:
time: 120 us; the launch traced here: 119 us
  Pallas kernels  117 us (98%)
  local copies, waits for them, and re-layouts  2.26 us (2%)
    pallas_call x1, Pallas kernels, per_device(): pl.pallas_call(kernel, out_shape=jax.ShapeDtypeStruct(matrix.shape, F32),...  117 us

profile of v10, /device:TPU:1, one launch (start us, length us, event | category | flops | bytes accessed | tf_op | source)
XLA Modules:
  0.0 119.5 jit_solution(9016928066101088454)
XLA Ops:
  0.0 117.2 %reduce_panels.1 = f32[512,512]{1,0:T(8,128)} custom-call(f32[512,512]{1,0:T(8,128)} %a_ref.1), custom_call_target="tpu_custom_call" | custom-call | tf_op jit(solution)/shard_map/reduce_panels/pallas_call | solution.py:668
  117.2 2.3 %copy.3 = f32[512,512]{1,0:T(8,128)} copy(f32[512,512]{1,0:T(8,128)} %reduce_panels.1) | data formatting | bytes 2097152
